TPU v7x, 32 devices: a whole 2x2x4 slice. The times are simulated.
32 devices in a mesh: groups: 2 (over x), chol: 16 (over z, y, core).
Axes of the slice: x: 2, y: 2, z: 4, core: 2. Of those that a mesh axis runs over, the one named last changes fastest.
Arguments:
- green_rows: bfloat16 [128, 65536], P('groups', 'chol'), parts along dimension 0, may hold values from -6 to 6
- factors: bfloat16 [5120, 65536], P(None, 'chol'), may hold values from -0.03125 to 0.03125
- noise_draws: float32 [128, 5120], P('groups', 'chol'), parts along dimension 0, may hold values from -6 to 6
Outputs:
- potential: float32 [128, 65536], P('groups', 'chol'), parts along dimension 0
- log_weight: float32 [128], P(('groups', 'chol')), parts along dimension 0
There are 2 independent parts, one for each index of `groups`. A program takes and returns all parts, laid end to end along the dimension named above; an argument that names none is the same for every part. Nothing has to cross between parts.
All inputs are finite; a program needn't handle non-finite values.
Results may differ from a plain program's by a relative error of at most 0.0029.
Values may be sent and summed in bfloat16 or wider, within the bound.
No kernel may reach another device: no remote copies, remote signals or barrier semaphores. Data moves between devices by JAX's collectives and lax.ppermute only.
A program may use at most 128 MiB of HBM per device.

v0:
```python
import math

import jax
import jax.numpy as jnp
from jax import lax
from jax.sharding import PartitionSpec as P


def forward(rows_in, factors):
    return lax.dot_general(
        rows_in, factors, (((1,), (1,)), ((), ())), preferred_element_type=jnp.float32
    )


def weights_of(fields, capped, total_vectors):
    return jnp.sum(fields * capped - 0.5 * capped * capped, axis=1) / math.sqrt(total_vectors)


def per_device(green_rows, factors, noise_draws):
    total_vectors = factors.shape[0]
    partial_value = forward(green_rows, factors)
    forces = lax.psum_scatter(partial_value, "chol", scatter_dimension=1, tiled=True)
    capped = jnp.tanh(forces)
    fields = noise_draws - capped
    log_weight = lax.psum_scatter(
        weights_of(fields, capped, total_vectors), "chol", scatter_dimension=0, tiled=True
    )
    field_low = fields.astype(jnp.bfloat16)
    potential = jnp.dot(
        lax.all_gather(field_low, "chol", axis=1, tiled=True),
        factors,
        preferred_element_type=jnp.float32,
    )
    return (potential, log_weight)


def solution(mesh):
    return jax.shard_map(
        per_device,
        mesh=mesh,
        in_specs=(P("groups", "chol"), P(None, "chol"), P("groups", "chol")),
        out_specs=(P("groups", "chol"), P(("groups", "chol"))),
        check_vma=False,
    )
```

profile of v0, /device:TPU:0, one launch (start us, length us, event | category | flops | bytes accessed | tf_op | source)
XLA Modules:
  0.0 172.4 jit_solution(7765970410692516359)
XLA Ops:
  7.2 0.0 copy-start
  7.2 0.0 copy-start.2
  7.2 0.0 copy-start.1
  7.2 0.0 reduce-scatter.4.cloned.1.call-start
  7.2 1.0 copy-done
  8.2 18.5 %convolution_bitcast_fusion = f32[5120,64]{1,0:T(8,128)} fusion(bf16[64,4096]{1,0:T(8,128)(2,1)S(1)} %copy-done, bf16[5120,4096]{1,0:T(8,128)(2,1)} %param.4), kind=kOutput, calls=%fused_computation | convolution fusion | flops 2684354560 | bytes 43778048
  26.7 0.0 reduce-scatter.4.cloned.1.call-update
  26.7 0.0 copy-done.2
  26.7 0.6 dynamic-slice
  28.0 65.8 %reduce-scatter.4.cloned.1.call-done = f32[320,64]{1,0:T(8,128)} async-done(((f32[5120,64]{1,0:T(8,128)}), f32[320,64]{1,0:T(8,128)}) %reduce-scatter.4.cloned.1.call-update) | async-done | bytes 81936
  93.8 1.0 copy.8
  94.8 0.0 copy-done.1
  94.8 0.1 fusion.1
  95.0 21.4 %all-gather = bf16[16,320,64]{1,2,0:T(8,128)(2,1)S(1)} all-gather(bf16[1,320,64]{1,2,0:T(8,128)(2,1)S(1)} %get-tuple-element.3), channel_id=1, replica_groups=mesh['groups'=2,'chol'=16] {'chol'}, dimensions={0}, use_global_device_ids=true | all-gather | bytes 696320 | tf_op jit(solution)/shard_map/all_gather | solution.py:30
  116.3 0.5 copy.6
  116.8 0.6 reshape.5
  117.4 17.7 %fusion.3 = f32[64,4096]{1,0:T(8,128)} fusion(bf16[5120,64]{0,1:T(8,128)(2,1)S(1)} %reshape.5, bf16[5120,4096]{1,0:T(8,128)(2,1)} %param.4), kind=kOutput, calls=%fused_computation.7 | convolution fusion | flops 2684354560 | bytes 43646976 | tf_op jit(solution)/shard_map/dot_general | solution.py:29
  135.1 29.8 %all-reduce = f32[64]{0:T(128)S(1)} all-reduce(f32[64]{0:T(128)S(1)} %broadcast_multiply_fusion), channel_id=3, replica_groups=mesh['groups'=2,'chol'=16] {'chol'}, use_global_device_ids=true, to_apply=%region_2.0.clone | all-reduce | flops 64 | bytes 512
  164.9 0.6 dynamic-slice.1
  (1 shorter events, 0.0 us)
Async XLA Ops:
  7.2 1.0 copy-start
  7.2 19.5 %copy-start.2 = (u32[32]{0:T(128)S(1)}, u32[32]{0:T(128)}, u32[]{:S(2)}) copy-start(u32[32]{0:T(128)} %constant.9) | copy-start | bytes 388
  7.2 87.6 %copy-start.1 = (f32[64,320]{1,0:T(8,128)S(1)}, f32[64,320]{1,0:T(8,128)}, u32[]{:S(2)}) copy-start(f32[64,320]{1,0:T(8,128)} %param.5) | copy-start | bytes 245764
  7.2 86.6 %reduce-scatter.4.cloned.1.call-start = ((), (), s32[]{:S(2)}) async-start(), calls=%async_computation.1 | async-start | bytes 2785280
Sparse Core Ops, SparseCore 0:
  26.8 66.9 reduce-scatter.3
where the time goes:
time: 173 us; the launch traced here: 172 us
  waiting for transfers between devices  65.8 us (38%)
  blocking collectives  51.2 us (30%)
  matrix products  36.1 us (21%)
  between operations  14.7 us (8%)
  local copies, waits for them, and re-layouts  4.26 us (2%)
    unnamed x2, waiting for transfers between devices  65.8 us
    unnamed x1, blocking collectives  29.8 us
    all_gather x1, blocking collectives, per_device(): lax.all_gather(field_low, 'chol', axis=1, tiled=True)  21.4 us
    unnamed x1, matrix products  18.5 us
    dot_general x1, matrix products, per_device(): jnp.dot(lax.all_gather(field_low, 'chol', axis=1, tiled=True), factors, p...  17.7 us
    unnamed x10, local copies, waits for them, and re-layouts  3.8 us
  transfers between devices with their start and end apart: 1, of which 1 were waited for; matrix products, arithmetic and copies ran while one was open for 0% of the time, Pallas kernels for 0%

commit v1 on v0

v1 whole, which is shorter than its diff:
```python
import functools
import math

import jax
import jax.numpy as jnp
from jax import lax
from jax.experimental import pallas as pl
from jax.experimental.pallas import tpu as pltpu
from jax.sharding import PartitionSpec as P

LANES = 128
TILE = 16
MARGIN = 4 * 1024 * 1024
SHARES = 4
BANKS = 4
HELD_BANKS = 4
VMEM = pl.BlockSpec(memory_space=pltpu.VMEM)
HBM = pl.BlockSpec(memory_space=pltpu.HBM)


def pack_rows(rows, pack):
    part = rows.shape[0] // pack
    return jnp.concatenate([rows[i * part : (i + 1) * part] for i in range(pack)], axis=1)


def unpack_rows(rows, pack):
    width = rows.shape[1] // pack
    return jnp.concatenate([rows[:, i * width : (i + 1) * width] for i in range(pack)], axis=0)


def params(limit=MARGIN):
    return pltpu.CompilerParams(vmem_limit_bytes=limit)


def share_of(owner, me):
    return lax.rem(owner, SHARES) ^ lax.rem(me, SHARES)


def forces_kernel(group, pack, rows_hbm, noise_hbm, slabs, kept, sent, draws, *refs):
    *banks, rows_in, noise, sems = refs
    n, size, pairs = slabs.shape
    depth = n // BANKS
    me = lax.axis_index("chol")

    def fetch(d, source, target):
        return pltpu.make_async_copy(source, target, sems.at[d])

    rows_copy = pltpu.make_async_copy(rows_hbm, rows_in, sems.at[n])
    rows_copy.start()
    noise_copy = pltpu.make_async_copy(noise_hbm, noise, sems.at[n + 1])
    noise_copy.start()
    for d in range(n):
        fetch(d, slabs.at[d], banks[d // depth].at[d % depth]).start()
    noise_copy.wait()
    draws[0] = pack_rows(noise[...].T, pack)
    rows_copy.wait()

    def step(source, offset, i, _):
        for j in range(group):
            fetch(i * group + j, slabs.at[i * group + j], source.at[i * group + j - offset]).wait()
        block = source[pl.ds(i * group - offset, group)].reshape(group * size, pairs)
        part = lax.dot_general(
            block, rows_in[...], (((1,), (1,)), ((), ())), preferred_element_type=jnp.float32
        )
        for j in range(group):
            owner = i * group + j
            share = share_of(owner, me)
            packed = pack_rows(part[j * size : (j + 1) * size], pack)

            @pl.when(share % 2 == 0)
            def _():
                kept[share // 2, owner // SHARES] = packed

            @pl.when(share % 2 == 1)
            def _():
                sent[share // 2, owner // SHARES] = packed.astype(sent.dtype)

    for b, bank in enumerate(banks):
        first = b * depth // group
        lax.fori_loop(first, first + depth // group, functools.partial(step, bank, b * depth), None)


def bank_bytes(slabs):
    return 2 * math.prod(slabs.shape) // BANKS


def forces_call(rows_in, noise, slabs, pack):
    walkers, pairs = rows_in.shape
    n, size, _ = slabs.shape
    half = (SHARES // 2, n // SHARES, size // pack, walkers * pack)
    bank = pltpu.VMEM((n // BANKS, size, pairs), jnp.bfloat16)
    n_rest = BANKS - HELD_BANKS
    return pl.pallas_call(
        functools.partial(forces_kernel, 2, pack),
        out_shape=(
            pltpu.VMEM(half, jnp.float32),
            pltpu.VMEM(half, jnp.bfloat16),
            pltpu.VMEM((1, *half[2:]), jnp.float32),
            *[bank] * HELD_BANKS,
        ),
        in_specs=[HBM, HBM, HBM],
        out_specs=(VMEM,) * (3 + HELD_BANKS),
        scratch_shapes=[
            *[bank] * n_rest,
            pltpu.VMEM(rows_in.shape, rows_in.dtype),
            pltpu.VMEM(noise.shape, noise.dtype),
            pltpu.SemaphoreType.DMA((n + 2,)),
        ],
        compiler_params=params(MARGIN + n_rest * bank_bytes(slabs)),
        cost_estimate=pl.CostEstimate(
            flops=2 * n * size * pairs * walkers, bytes_accessed=2 * n * size * pairs, transcendentals=0
        ),
    )(*(pltpu.with_memory_space_constraint(x, pltpu.HBM) for x in (rows_in, noise, slabs)))


def split_kernel(kept, received, out, sent):
    out[...] = kept[0] + received[0].astype(jnp.float32)
    sent[...] = (kept[1] + received[1].astype(jnp.float32)).astype(sent.dtype)


def split_call(kept, received):
    return pl.pallas_call(
        split_kernel,
        out_shape=(pltpu.VMEM(kept.shape[1:], kept.dtype), pltpu.VMEM(kept.shape[1:], received.dtype)),
        in_specs=[VMEM] * 2,
        out_specs=(VMEM, VMEM),
        compiler_params=params(),
    )(kept, received)


def add_kernel(kept, received, out, sent):
    total = kept[...] + received[...].astype(jnp.float32)
    out[...] = total
    sent[...] = total.astype(sent.dtype)


def add_call(kept, received):
    return pl.pallas_call(
        add_kernel,
        out_shape=(pltpu.VMEM(kept.shape, kept.dtype), pltpu.VMEM(kept.shape, received.dtype)),
        in_specs=[VMEM] * 2,
        out_specs=(VMEM, VMEM),
        compiler_params=params(),
    )(kept, received)


def join_kernel(first, second, out):
    part = first.shape[0]
    out[:part] = first[...]
    out[part:] = second[...]


def join_call(first, second):
    return pl.pallas_call(
        join_kernel,
        out_shape=pltpu.VMEM((2 * first.shape[0], *first.shape[1:]), first.dtype),
        in_specs=[VMEM] * 2,
        out_specs=VMEM,
        compiler_params=params(),
    )(first, second)


def place_of(difference, n_high):
    place = 0
    for b in range(n_high.bit_length() - 1):
        place += ((difference >> b) & 1) * (n_high >> (b + 1))
    return place


def fields_kernel(kept, received, noise, out):
    n_high, rows, lanes = kept.shape
    me = lax.axis_index("chol")
    terms = jnp.zeros((1, lanes), jnp.float32)
    for z in range(n_high):
        capped = jnp.tanh(kept[z] + received[z].astype(jnp.float32))
        fields = noise[place_of(z ^ (me // SHARES), n_high)] - capped
        terms += jnp.sum(fields * capped - 0.5 * capped * capped, axis=0, keepdims=True)
        out[z * rows : (z + 1) * rows] = fields.astype(jnp.bfloat16)
    high = terms.astype(jnp.bfloat16).astype(jnp.float32)
    mid = (terms - high).astype(jnp.bfloat16).astype(jnp.float32)
    low = terms - high - mid
    row = lax.broadcasted_iota(jnp.int32, (TILE, lanes), 0)
    tail = jnp.where(row == 0, high, jnp.where(row == 1, mid, jnp.where(row == 2, low, 0.0)))
    out[n_high * rows :] = tail.astype(jnp.bfloat16)


def fields_call(kept, received, noise):
    n_high, rows, lanes = kept.shape
    return pl.pallas_call(
        fields_kernel,
        out_shape=jax.ShapeDtypeStruct((n_high * rows + TILE, lanes), jnp.bfloat16),
        in_specs=[VMEM] * 3,
        out_specs=VMEM,
        compiler_params=params(),
    )(kept, received, noise)


def potential_kernel(shares, pack, last, scale, *refs):
    pieces = refs[: len(shares)]
    refs = refs[len(shares) :]
    if last:
        earlier, refs = refs[:2], refs[2:]
    banks, refs = refs[:HELD_BANKS], refs[HELD_BANKS:]
    if last:
        slabs, before, out, weight, rest, sems = refs
    else:
        slabs, out, rest, sems = refs
    me = lax.axis_index("chol")
    n, size, _ = slabs.shape
    rows = size // pack
    n_high = n // SHARES
    depth = n_high // BANKS
    z_held = depth * HELD_BANKS
    spots = [share ^ lax.rem(me, SHARES) for share in shares]
    left = [(k, z) for k in range(len(shares)) for z in range(z_held, n_high)]

    def fetch(slot):
        k, z = left[slot]
        return pltpu.make_async_copy(slabs.at[z * SHARES + spots[k]], rest.at[slot], sems.at[slot])

    for slot in range(len(left)):
        fetch(slot).start()
    out[...] = before[...] if last else jnp.zeros_like(out)

    def add(piece, z, block):
        fields = unpack_rows(piece[pl.ds(pl.multiple_of(z * rows, TILE), rows)], pack)
        out[...] += lax.dot_general(
            fields, block, (((0,), (0,)), ((), ())), preferred_element_type=jnp.float32
        )

    def add_bank(b, bank, z, _):
        for spot, piece in zip(spots, pieces):
            add(piece, b * depth + z, bank[z * SHARES + spot])

    for b, bank in enumerate(banks):
        lax.fori_loop(0, depth, functools.partial(add_bank, b, bank), None)
    for slot, (k, z) in enumerate(left):
        fetch(slot).wait()
        add(pieces[k], z, rest[slot])
    if last:
        walkers = out.shape[0]
        terms = sum(
            jnp.sum(p[n_high * rows :].astype(jnp.float32), axis=0, keepdims=True)
            for p in (*pieces, *earlier)
        )
        lanes = terms.shape[1]
        whole = terms
        for i in range(1, pack):
            whole = whole + pltpu.roll(terms, i * walkers, 1)
        mine = walkers // n
        shift = lax.rem(lanes - me * mine, lanes)
        weight[...] = (pltpu.roll(jnp.broadcast_to(whole, (8, lanes)), shift, 1) * scale)[:1, :mine]


def potential_call(shares, pieces, earlier, banks, slabs, before, walkers, pack, scale):
    n, size, pairs = slabs.shape
    n_rest = n // BANKS * (BANKS - HELD_BANKS) * len(shares) // SHARES
    rest = (max(1, n_rest), size if n_rest else TILE, pairs)
    last = before is not None
    out = jax.ShapeDtypeStruct((walkers, pairs), jnp.float32)
    weight = jax.ShapeDtypeStruct((1, walkers // n), jnp.float32)
    banks = [pltpu.with_memory_space_constraint(bank, pltpu.VMEM) for bank in banks]
    slabs = pltpu.with_memory_space_constraint(slabs, pltpu.HBM)
    args = (*pieces, *earlier, *banks, slabs, before) if last else (*pieces, *banks, slabs)
    specs = [HBM if arg is slabs else VMEM for arg in args]
    work = n * size * len(shares) // SHARES
    return pl.pallas_call(
        functools.partial(potential_kernel, shares, pack, last, scale),
        out_shape=(out, weight) if last else out,
        in_specs=specs,
        out_specs=(VMEM, VMEM) if last else VMEM,
        scratch_shapes=[pltpu.VMEM(rest, jnp.bfloat16), pltpu.SemaphoreType.DMA((max(1, n_rest),))],
        compiler_params=params(MARGIN + 2 * math.prod(rest)),
        cost_estimate=pl.CostEstimate(
            flops=2 * work * pairs * walkers, bytes_accessed=2 * work * pairs, transcendentals=0
        ),
    )(*args)


def swap(block, bit, n):
    return lax.ppermute(block, "chol", [(i, i ^ bit) for i in range(n)])


def per_device(green_rows, factors, noise_draws):
    walkers = green_rows.shape[0]
    vectors, pairs = factors.shape
    n = lax.axis_size("chol")
    own = vectors // n
    pack = max(1, LANES // walkers)
    scale = 1.0 / math.sqrt(vectors)
    slabs = factors.reshape(n, own, pairs)
    high_bits = [1 << b for b in range(2, n.bit_length() - 1)]

    kept, sent, noise, *banks = forces_call(green_rows, noise_draws, slabs, pack)
    forces, sent = split_call(kept, swap(sent, 1, n))
    received = swap(sent, 2, n)
    for i, bit in enumerate(high_bits):
        noise = join_call(noise, swap(noise, high_bits[-1 - i], n))
        forces, sent = add_call(forces, received)
        received = swap(sent, bit, n)
    own_fields = fields_call(forces, received, noise)
    across = swap(own_fields, 2, n)
    beside = swap(own_fields, 1, n)
    pieces = (own_fields, beside)
    potential = potential_call((0, 1), pieces, (), banks, slabs, None, walkers, pack, scale)
    beyond = swap(across, 1, n)
    potential, weight = potential_call(
        (2, 3), (across, beyond), pieces, banks, slabs, potential, walkers, pack, scale
    )
    return (potential, weight.reshape(-1))


def solution(mesh):
    return jax.shard_map(
        per_device,
        mesh=mesh,
        in_specs=(P("groups", "chol"), P(None, "chol"), P("groups", "chol")),
        out_specs=(P("groups", "chol"), P(("groups", "chol"))),
        check_vma=False,
    )
```

time: 173 us -> 59.6 us (0.34)
  blocking collectives: 51.2 us -> 0 us
  waiting for transfers between devices: 65.8 us -> 19.8 us
  matrix products: 36.1 us -> 0 us
  Pallas kernels: 0 us -> 25.6 us
  between operations: 14.7 us -> 0.68 us
  starting transfers between devices: 0.04 us -> 13.4 us
  local copies, waits for them, and re-layouts: 4.26 us -> 0 us
    unnamed x2 -> x0, waiting for transfers between devices: 65.8 us -> none
    unnamed x1 -> x0, blocking collectives: 29.8 us -> none
    pallas_call x0 -> x9, Pallas kernels: none -> 25.6 us  [the longest x1 15.8 us: forces_call(): pl.pallas_call(functools.partial(forces_kernel, 2, pack), out_shape=(pltp...]
    all_gather x1 -> x0, blocking collectives: 21.4 us -> none  [per_device(): lax.all_gather(field_low, 'chol', axis=1, tiled=True)]
    ppermute x0 -> x9, waiting for transfers between devices: none -> 19.8 us  [swap(): return lax.ppermute(block, 'chol', [(i, i ^ bit) for i in range(n)])]
    unnamed x1 -> x0, matrix products: 18.5 us -> none
    dot_general x1 -> x0, matrix products: 17.7 us -> none  [per_device(): jnp.dot(lax.all_gather(field_low, 'chol', axis=1, tiled=True), factors, p...]
    ppermute x0 -> x9, starting transfers between devices: none -> 13.4 us  [swap(): return lax.ppermute(block, 'chol', [(i, i ^ bit) for i in range(n)])]
  transfers between devices with their start and end apart: 1 -> 9, of which waited for: 1 -> 6; matrix products, arithmetic and copies ran while one was open for 0% -> 0% of each run, Pallas kernels for 0% -> 7%
where the time goes in v1:
time: 59.6 us; the launch traced here: 59.4 us
  Pallas kernels  25.6 us (43%)
  waiting for transfers between devices  19.8 us (33%)
  starting transfers between devices  13.4 us (22%)
  between operations  0.68 us (1%)
    ppermute x9, waiting for transfers between devices, swap(): return lax.ppermute(block, 'chol', [(i, i ^ bit) for i in range(n)])  19.8 us
    pallas_call x1, Pallas kernels, forces_call(): pl.pallas_call(functools.partial(forces_kernel, 2, pack), out_shape=(pltp...  15.8 us
    ppermute x9, starting transfers between devices, swap(): return lax.ppermute(block, 'chol', [(i, i ^ bit) for i in range(n)])  13.4 us
    pallas_call x2, Pallas kernels, potential_call(): pl.pallas_call(functools.partial(potential_kernel, shares, pack, last, sc...  9.51 us
  transfers between devices with their start and end apart: 9, of which 6 were waited for; matrix products, arithmetic and copies ran while one was open for 0% of the time, Pallas kernels for 7%

profile of v1, /device:TPU:0, one launch (start us, length us, event | category | flops | bytes accessed | tf_op | source)
XLA Modules:
  0.0 59.4 jit_solution(12897454441935956003)
XLA Ops:
  0.6 15.8 %shard_map.50 = (f32[2,4,160,128]{3,2,1,0:T(8,128)S(1)}, bf16[2,4,160,128]{3,2,1,0:T(8,128)(2,1)S(1)}, f32[1,160,128]{2,1,0:T(8,128)S(1)}, bf16[4,320,4096]{2,1,...) custom-call(bf16[64,4096]{1,0:T(8,128)(2,1)} %rows_hbm.1, ...), custom_call_target="tpu_custom_call" | custom-call | flops 2684354560 | bytes 41943040 | tf_op jit(solution)/shard_map/pallas_call | solution.py:93
  16.4 0.6 collective-permute-start
  17.0 1.3 %collective-permute-done.received = bf16[2,4,160,128]{3,2,1,0:T(8,128)(2,1)S(1)} collective-permute-done((bf16[2,4,160,128]{3,2,1,0:T(8,128)(2,1)S(1)}, bf16[2,4,160,128]{3,2,1,0:T(8,128)(2,1)S(1)}, u32[]{:S(2)}, u32[]{:S(2)}) %collective-permute-start) | collective-permute-done | bytes 327712 | tf_op jit(solution)/shard_map/ppermute | solution.py:281
  18.2 0.1 shard_map.51
  18.3 2.9 %collective-permute-start.1 = (bf16[4,160,128]{2,1,0:T(8,128)(2,1)S(1)}, bf16[4,160,128]{2,1,0:T(8,128)(2,1)S(1)}, u32[]{:S(2)}, u32[]{:S(2)}) collective-permute-start(bf16[4,160,128]{2,1,0:T(8,128)(2,1)S(1)} %get-tuple-element.20), channel_id=1, source_target_pairs={{0,2},{1,3},{2,0},{3,1},{4,6},{5,7},{6,4},{7,5},{8,10},{9,11},{10,... | collective-permute-start | bytes 491528 | tf_op jit(solution)/shard_map/ppermute | solution.py:281
  21.2 4.5 %collective-permute-done.1.received = bf16[4,160,128]{2,1,0:T(8,128)(2,1)S(1)} collective-permute-done((bf16[4,160,128]{2,1,0:T(8,128)(2,1)S(1)}, bf16[4,160,128]{2,1,0:T(8,128)(2,1)S(1)}, u32[]{:S(2)}, u32[]{:S(2)}) %collective-permute-start.1) | collective-permute-done | bytes 163872 | tf_op jit(solution)/shard_map/ppermute | solution.py:281
  25.8 1.9 %collective-permute-start.2 = (bf16[4,160,128]{2,1,0:T(8,128)(2,1)S(1)}, bf16[4,160,128]{2,1,0:T(8,128)(2,1)S(1)}, u32[]{:S(2)}, u32[]{:S(2)}) collective-permute-start(bf16[4,160,128]{2,1,0:T(8,128)(2,1)S(1)} %get-tuple-element.22), channel_id=1, source_target_pairs={{0,4},{1,5},{2,6},{3,7},{4,0},{5,1},{6,2},{7,3},{8,12},{9,13},{10,... | collective-permute-start | bytes 491528 | tf_op jit(solution)/shard_map/ppermute | solution.py:281
  27.6 2.6 %collective-permute-start.4 = (f32[1,160,128]{2,1,0:T(8,128)S(1)}, f32[1,160,128]{2,1,0:T(8,128)S(1)}, u32[]{:S(2)}, u32[]{:S(2)}) collective-permute-start(f32[1,160,128]{2,1,0:T(8,128)S(1)} %get-tuple-element.25.first), channel_id=1, source_target_pairs={{0,8},{1,9},{2,10},{3,11},{4,12},{5,13},{6,14},{7,15},{8,0},{9,1},... | collective-permute-start | bytes 245768 | tf_op jit(solution)/shard_map/ppermute | solution.py:281
  30.2 3.5 %collective-permute-done.4.second = f32[1,160,128]{2,1,0:T(8,128)S(1)} collective-permute-done((f32[1,160,128]{2,1,0:T(8,128)S(1)}, f32[1,160,128]{2,1,0:T(8,128)S(1)}, u32[]{:S(2)}, u32[]{:S(2)}) %collective-permute-start.4) | collective-permute-done | bytes 81952 | tf_op jit(solution)/shard_map/ppermute | solution.py:281
  33.7 2.2 %collective-permute-start.5 = (f32[2,160,128]{2,1,0:T(8,128)S(1)}, f32[2,160,128]{2,1,0:T(8,128)S(1)}, u32[]{:S(2)}, u32[]{:S(2)}) collective-permute-start(f32[2,160,128]{2,1,0:T(8,128)S(1)} %shard_map.54.first), channel_id=1, source_target_pairs={{0,4},{1,5},{2,6},{3,7},{4,0},{5,1},{6,2},{7,3},{8,12},{9,13},{10,... | collective-permute-start | bytes 491528 | tf_op jit(solution)/shard_map/ppermute | solution.py:281
  35.9 0.0 collective-permute-done.2.received
  35.9 1.7 %collective-permute-start.3 = (bf16[4,160,128]{2,1,0:T(8,128)(2,1)S(1)}, bf16[4,160,128]{2,1,0:T(8,128)(2,1)S(1)}, u32[]{:S(2)}, u32[]{:S(2)}) collective-permute-start(bf16[4,160,128]{2,1,0:T(8,128)(2,1)S(1)} %get-tuple-element.24), channel_id=1, source_target_pairs={{0,8},{1,9},{2,10},{3,11},{4,12},{5,13},{6,14},{7,15},{8,0},{9,1},... | collective-permute-start | bytes 491528 | tf_op jit(solution)/shard_map/ppermute | solution.py:281
  37.6 3.4 %collective-permute-done.5.second = f32[2,160,128]{2,1,0:T(8,128)S(1)} collective-permute-done((f32[2,160,128]{2,1,0:T(8,128)S(1)}, f32[2,160,128]{2,1,0:T(8,128)S(1)}, u32[]{:S(2)}, u32[]{:S(2)}) %collective-permute-start.5) | collective-permute-done | bytes 163872 | tf_op jit(solution)/shard_map/ppermute | solution.py:281
  41.0 3.4 %collective-permute-done.3.received = bf16[4,160,128]{2,1,0:T(8,128)(2,1)S(1)} collective-permute-done((bf16[4,160,128]{2,1,0:T(8,128)(2,1)S(1)}, bf16[4,160,128]{2,1,0:T(8,128)(2,1)S(1)}, u32[]{:S(2)}, u32[]{:S(2)}) %collective-permute-start.3) | collective-permute-done | bytes 163872 | tf_op jit(solution)/shard_map/ppermute | solution.py:281
  44.4 0.1 shard_map.56.refs_0_.refs_2_
  44.5 1.6 %collective-permute-start.6 = (bf16[656,128]{1,0:T(8,128)(2,1)S(1)}, bf16[656,128]{1,0:T(8,128)(2,1)S(1)}, u32[]{:S(2)}, u32[]{:S(2)}) collective-permute-start(bf16[656,128]{1,0:T(8,128)(2,1)S(1)} %shard_map.56.refs_0_.refs_2_), channel_id=1, source_target_pairs={{0,2},{1,3},{2,0},{3,1},{4,6},{5,7},{6,4},{7,5},{8,10},{9,11},{10,... | collective-permute-start | bytes 503816 | tf_op jit(solution)/shard_map/ppermute | solution.py:281
  46.1 0.0 collective-permute-start.8
  46.1 3.8 %collective-permute-done.6.refs_0_ = bf16[656,128]{1,0:T(8,128)(2,1)S(1)} collective-permute-done((bf16[656,128]{1,0:T(8,128)(2,1)S(1)}, bf16[656,128]{1,0:T(8,128)(2,1)S(1)}, u32[]{:S(2)}, u32[]{:S(2)}) %collective-permute-start.6) | collective-permute-done | bytes 167968 | tf_op jit(solution)/shard_map/ppermute | solution.py:281
  49.9 0.0 collective-permute-start.7
  49.9 0.0 collective-permute-done.8.refs_1_.refs_3_
  49.9 4.3 %shard_map.57.refs_9_ = f32[64,4096]{1,0:T(8,128)S(1)} custom-call(bf16[656,128]{1,0:T(8,128)(2,1)S(1)} %shard_map.56.refs_0_.refs_2_, bf16[656,128]{1,0:T(8,128)(2,1)S(1)} %collective-permute-done.8.refs_1_.refs_3_, bf16[4,320,4096]{2,1,0:T(8,128)(2,1)S(1)} %get-tuple-element.26.refs_2_.refs_4_, ...), custom_call_target="tpu_custom_call" | custom-call | flops 1342177280 | bytes 20971520 | tf_op jit(solution)/shard_map/pallas_call | solution.py:267
  54.2 0.0 collective-permute-done.7.refs_1_
  54.2 5.2 %shard_map.58 = (f32[64,4096]{1,0:T(8,128)}, f32[1,4]{1,0:T(1,128)}) custom-call(bf16[656,128]{1,0:T(8,128)(2,1)S(1)} %collective-permute-done.6.refs_0_, bf16[656,128]{1,0:T(8,128)(2,1)S(1)} %collective-permute-done.7.refs_1_, bf16[656,128]{1,0:T(8,128)(2,1)S(1)} %shard_map.56.refs_0_.refs_2_, bf16[656,128]{1,0:T(8,128)(2,1)S(1)} %collective-permute-done.8.refs_1_.refs_3_, ...), custom_call_target="tpu_custom_call" | custom-call | flops 1342177280 | bytes 20971520 | tf_op jit(solution)/shard_map/pallas_call | solution.py:267
  (4 shorter events, 0.1 us)
Async XLA Ops:
  16.4 1.8 %collective-permute-start = (bf16[2,4,160,128]{3,2,1,0:T(8,128)(2,1)S(1)}, bf16[2,4,160,128]{3,2,1,0:T(8,128)(2,1)S(1)}, u32[]{:S(2)}, u32[]{:S(2)}) collective-permute-start(bf16[2,4,160,128]{3,2,1,0:T(8,128)(2,1)S(1)} %get-tuple-element.18), channel_id=1, source_target_pairs={{0,1},{1,0},{2,3},{3,2},{4,5},{5,4},{6,7},{7,6},{8,9},{9,8},{10,11... | collective-permute-start | bytes 983048 | tf_op jit(solution)/shard_map/ppermute | solution.py:281
  18.3 7.4 %collective-permute-start.1 = (bf16[4,160,128]{2,1,0:T(8,128)(2,1)S(1)}, bf16[4,160,128]{2,1,0:T(8,128)(2,1)S(1)}, u32[]{:S(2)}, u32[]{:S(2)}) collective-permute-start(bf16[4,160,128]{2,1,0:T(8,128)(2,1)S(1)} %get-tuple-element.20), channel_id=1, source_target_pairs={{0,2},{1,3},{2,0},{3,1},{4,6},{5,7},{6,4},{7,5},{8,10},{9,11},{10,... | collective-permute-start | bytes 491528 | tf_op jit(solution)/shard_map/ppermute | solution.py:281
  25.8 10.1 %collective-permute-start.2 = (bf16[4,160,128]{2,1,0:T(8,128)(2,1)S(1)}, bf16[4,160,128]{2,1,0:T(8,128)(2,1)S(1)}, u32[]{:S(2)}, u32[]{:S(2)}) collective-permute-start(bf16[4,160,128]{2,1,0:T(8,128)(2,1)S(1)} %get-tuple-element.22), channel_id=1, source_target_pairs={{0,4},{1,5},{2,6},{3,7},{4,0},{5,1},{6,2},{7,3},{8,12},{9,13},{10,... | collective-permute-start | bytes 491528 | tf_op jit(solution)/shard_map/ppermute | solution.py:281
  27.6 6.1 %collective-permute-start.4 = (f32[1,160,128]{2,1,0:T(8,128)S(1)}, f32[1,160,128]{2,1,0:T(8,128)S(1)}, u32[]{:S(2)}, u32[]{:S(2)}) collective-permute-start(f32[1,160,128]{2,1,0:T(8,128)S(1)} %get-tuple-element.25.first), channel_id=1, source_target_pairs={{0,8},{1,9},{2,10},{3,11},{4,12},{5,13},{6,14},{7,15},{8,0},{9,1},... | collective-permute-start | bytes 245768 | tf_op jit(solution)/shard_map/ppermute | solution.py:281
  33.7 7.2 %collective-permute-start.5 = (f32[2,160,128]{2,1,0:T(8,128)S(1)}, f32[2,160,128]{2,1,0:T(8,128)S(1)}, u32[]{:S(2)}, u32[]{:S(2)}) collective-permute-start(f32[2,160,128]{2,1,0:T(8,128)S(1)} %shard_map.54.first), channel_id=1, source_target_pairs={{0,4},{1,5},{2,6},{3,7},{4,0},{5,1},{6,2},{7,3},{8,12},{9,13},{10,... | collective-permute-start | bytes 491528 | tf_op jit(solution)/shard_map/ppermute | solution.py:281
  35.9 8.4 %collective-permute-start.3 = (bf16[4,160,128]{2,1,0:T(8,128)(2,1)S(1)}, bf16[4,160,128]{2,1,0:T(8,128)(2,1)S(1)}, u32[]{:S(2)}, u32[]{:S(2)}) collective-permute-start(bf16[4,160,128]{2,1,0:T(8,128)(2,1)S(1)} %get-tuple-element.24), channel_id=1, source_target_pairs={{0,8},{1,9},{2,10},{3,11},{4,12},{5,13},{6,14},{7,15},{8,0},{9,1},... | collective-permute-start | bytes 491528 | tf_op jit(solution)/shard_map/ppermute | solution.py:281
  44.5 5.4 %collective-permute-start.6 = (bf16[656,128]{1,0:T(8,128)(2,1)S(1)}, bf16[656,128]{1,0:T(8,128)(2,1)S(1)}, u32[]{:S(2)}, u32[]{:S(2)}) collective-permute-start(bf16[656,128]{1,0:T(8,128)(2,1)S(1)} %shard_map.56.refs_0_.refs_2_), channel_id=1, source_target_pairs={{0,2},{1,3},{2,0},{3,1},{4,6},{5,7},{6,4},{7,5},{8,10},{9,11},{10,... | collective-permute-start | bytes 503816 | tf_op jit(solution)/shard_map/ppermute | solution.py:281
  46.1 3.8 %collective-permute-start.8 = (bf16[656,128]{1,0:T(8,128)(2,1)S(1)}, bf16[656,128]{1,0:T(8,128)(2,1)S(1)}, u32[]{:S(2)}, u32[]{:S(2)}) collective-permute-start(bf16[656,128]{1,0:T(8,128)(2,1)S(1)} %shard_map.56.refs_0_.refs_2_), channel_id=1, source_target_pairs={{0,1},{1,0},{2,3},{3,2},{4,5},{5,4},{6,7},{7,6},{8,9},{9,8},{10,11... | collective-permute-start | bytes 503816 | tf_op jit(solution)/shard_map/ppermute | solution.py:281
  49.9 4.3 %collective-permute-start.7 = (bf16[656,128]{1,0:T(8,128)(2,1)S(1)}, bf16[656,128]{1,0:T(8,128)(2,1)S(1)}, u32[]{:S(2)}, u32[]{:S(2)}) collective-permute-start(bf16[656,128]{1,0:T(8,128)(2,1)S(1)} %collective-permute-done.6.refs_0_), channel_id=1, source_target_pairs={{0,1},{1,0},{2,3},{3,2},{4,5},{5,4},{6,7},{7,6},{8,9},{9,8},{10,11... | collective-permute-start | bytes 503816 | tf_op jit(solution)/shard_map/ppermute | solution.py:281

commit v2 on v0

v2 whole, which is shorter than its diff:
```python
import functools
import math

import jax
import jax.numpy as jnp
from jax import lax
from jax.experimental import pallas as pl
from jax.experimental.pallas import tpu as pltpu
from jax.sharding import PartitionSpec as P

LANES = 128
TILE = 16
MARGIN = 4 * 1024 * 1024
SHARES = 8
BANKS = 4
COLUMNS = 1024
WIRE = jnp.float16
VMEM = pl.BlockSpec(memory_space=pltpu.VMEM)
HBM = pl.BlockSpec(memory_space=pltpu.HBM)


def params(limit=MARGIN):
    return pltpu.CompilerParams(vmem_limit_bytes=limit)


def bands_of(size):
    units = size // TILE
    ends = [-(-units * (b + 1) // BANKS) * TILE for b in range(BANKS)]
    return tuple(zip([0, *ends], ends))


def pack_rows(rows, pack):
    part = rows.shape[0] // pack
    return jnp.concatenate([rows[i * part : (i + 1) * part] for i in range(pack)], axis=1)


def unpack_rows(rows, pack):
    width = rows.shape[1] // pack
    return jnp.concatenate([rows[:, i * width : (i + 1) * width] for i in range(pack)], axis=0)


def share_of(owner, me):
    return lax.rem(owner, SHARES) ^ lax.rem(me, SHARES)


def forces_kernel(bands, pack, rows_hbm, noise_hbm, slabs, kept, sent, draws, *refs):
    *banks, rows_in, noise, sems = refs
    n, size, _ = slabs.shape
    me = lax.axis_index("chol")

    def fetch(d, b):
        lo, hi = bands[b]
        return pltpu.make_async_copy(slabs.at[d, lo:hi], banks[b].at[d], sems.at[d * BANKS + b])

    rows_copy = pltpu.make_async_copy(rows_hbm, rows_in, sems.at[n * BANKS])
    rows_copy.start()
    for d in range(n):
        for b in range(BANKS):
            fetch(d, b).start()
    noise_copy = pltpu.make_async_copy(noise_hbm, noise, sems.at[n * BANKS + 1])
    noise_copy.start()
    rows_copy.wait()

    def step(group, i, _):
        parts = []
        for j in range(group):
            for b in range(BANKS):
                fetch(i * group + j, b).wait()
        for j in range(group):
            parts += [bank[i * group + j] for bank in banks]
        part = lax.dot_general(
            jnp.concatenate(parts, axis=0),
            rows_in[...],
            (((1,), (1,)), ((), ())),
            preferred_element_type=jnp.float32,
        )
        for j in range(group):
            owner = i * group + j
            share = share_of(owner, me)
            packed = pack_rows(part[j * size : (j + 1) * size], pack)

            @pl.when(share % 2 == 0)
            def _():
                kept[share // 2, owner // SHARES] = packed

            @pl.when(share % 2 == 1)
            def _():
                sent[share // 2, owner // SHARES] = packed

    lax.fori_loop(0, n // 2 - 1, functools.partial(step, 2), None)
    lax.fori_loop(n - 2, n, functools.partial(step, 1), None)
    noise_copy.wait()
    draws[0] = pack_rows(noise[...].T, pack)


def forces_call(rows_in, noise, slabs, bands, pack):
    walkers, pairs = rows_in.shape
    n, size, _ = slabs.shape
    half = (SHARES // 2, n // SHARES, size // pack, walkers * pack)
    return pl.pallas_call(
        functools.partial(forces_kernel, bands, pack),
        out_shape=(
            pltpu.VMEM(half, jnp.float32),
            pltpu.VMEM(half, jnp.float32),
            pltpu.VMEM((1, *half[2:]), jnp.float32),
            *[pltpu.VMEM((n, hi - lo, pairs), jnp.bfloat16) for lo, hi in bands],
        ),
        in_specs=[HBM, HBM, HBM],
        out_specs=(VMEM,) * (3 + BANKS),
        scratch_shapes=[
            pltpu.VMEM(rows_in.shape, rows_in.dtype),
            pltpu.VMEM(noise.shape, noise.dtype),
            pltpu.SemaphoreType.DMA((n * BANKS + 2,)),
        ],
        compiler_params=params(),
        cost_estimate=pl.CostEstimate(
            flops=2 * n * size * pairs * walkers, bytes_accessed=2 * n * size * pairs, transcendentals=0
        ),
    )(*(pltpu.with_memory_space_constraint(x, pltpu.HBM) for x in (rows_in, noise, slabs)))


def small_call(kernel, outs, *args):
    return pl.pallas_call(
        kernel,
        out_shape=[pltpu.VMEM(shape, jnp.float32) for shape in outs],
        in_specs=[VMEM] * len(args),
        out_specs=[VMEM] * len(outs),
        compiler_params=params(),
    )(*args)


def split_kernel(kept, received, out, sent):
    for i in range(out.shape[0]):
        out[i] = kept[2 * i] + received[2 * i]
        sent[i] = kept[2 * i + 1] + received[2 * i + 1]


def add_kernel(kept, received, out):
    out[...] = kept[...] + received[...]


def join_kernel(first, second, out):
    part = first.shape[0]
    out[:part] = first[...]
    out[part:] = second[...]


def place_of(difference, n_high):
    place = 0
    for b in range(n_high.bit_length() - 1):
        place += ((difference >> b) & 1) * (n_high >> (b + 1))
    return place


def fields_kernel(kept, received, noise, out):
    n_high, rows, lanes = kept.shape
    me = lax.axis_index("chol")
    terms = jnp.zeros((1, lanes), jnp.float32)
    for z in range(n_high):
        capped = jnp.tanh(kept[z] + received[z])
        fields = noise[place_of(z ^ (me // SHARES), n_high)] - capped
        terms += jnp.sum(fields * capped - 0.5 * capped * capped, axis=0, keepdims=True)
        out[z * rows : (z + 1) * rows] = fields.astype(jnp.bfloat16)
    high = terms.astype(jnp.bfloat16).astype(jnp.float32)
    mid = (terms - high).astype(jnp.bfloat16).astype(jnp.float32)
    low = terms - high - mid
    row = lax.broadcasted_iota(jnp.int32, (TILE, lanes), 0)
    tail = jnp.where(row == 0, high, jnp.where(row == 1, mid, jnp.where(row == 2, low, 0.0)))
    out[n_high * rows :] = tail.astype(jnp.bfloat16)


def fields_call(kept, received, noise):
    n_high, rows, lanes = kept.shape
    return pl.pallas_call(
        fields_kernel,
        out_shape=pltpu.VMEM((n_high * rows + TILE, lanes), jnp.bfloat16),
        in_specs=[VMEM] * 3,
        out_specs=VMEM,
        compiler_params=params(),
    )(kept, received, noise)


def potential_kernel(shares, pack, first, last, scale, *refs):
    pieces, refs = refs[: len(shares)], refs[len(shares) :]
    if last:
        earlier, refs = refs[: SHARES - len(shares)], refs[SHARES - len(shares) :]
    banks, refs = refs[:BANKS], refs[BANKS:]
    if not first:
        before, *refs = refs
    if last:
        out, weight, total, mine, sems = refs
    else:
        (total,) = refs
    me = lax.axis_index("chol")
    n = banks[0].shape[0]
    n_high = n // SHARES
    rows = pieces[0].shape[0] // n_high // TILE * TILE
    walkers, pairs = total.shape
    width = min(COLUMNS, pairs)
    blocks = pairs // width

    def store(j):
        cols = pl.ds(j * width, width)
        return pltpu.make_async_copy(total.at[:, cols], out.at[:, cols], sems.at[j])

    weight_copy = pltpu.make_async_copy(mine, weight, sems.at[blocks]) if last else None
    if last:
        terms = sum(
            jnp.sum(p[n_high * rows :].astype(jnp.float32), axis=0, keepdims=True)
            for p in (*pieces, *earlier)
        )
        lanes = terms.shape[1]
        whole = terms
        for i in range(1, pack):
            whole = whole + pltpu.roll(terms, i * walkers, 1)
        shift = lax.rem(lanes - me * (walkers // n), lanes)
        rolled = pltpu.roll(jnp.broadcast_to(whole, (8, lanes)), shift, 1) * scale
        mine[...] = rolled[:1, : walkers // n]
        weight_copy.start()
    fields, places = [], []
    for share, piece in zip(shares, pieces):
        for z in range(n_high):
            fields.append(unpack_rows(piece[z * rows : (z + 1) * rows], pack))
            places.append(z * SHARES + (share ^ lax.rem(me, SHARES)))
    columns = jnp.concatenate(fields, axis=0)
    for j in range(blocks):
        cols = slice(j * width, (j + 1) * width)
        block = jnp.concatenate([bank[at, :, cols] for at in places for bank in banks], axis=0)
        part = lax.dot_general(
            columns, block, (((0,), (0,)), ((), ())), preferred_element_type=jnp.float32
        )
        total[:, cols] = part if first else before[:, cols] + part
        if last:
            store(j).start()
    if last:
        weight_copy.wait()
        for j in range(blocks):
            store(j).wait()


def potential_call(shares, pieces, earlier, banks, before, walkers, pack, scale):
    n, _, pairs = banks[0].shape
    first, last = before is None, bool(earlier)
    total = pltpu.VMEM((walkers, pairs), jnp.float32)
    mine = pltpu.VMEM((1, walkers // n), jnp.float32)
    out = jax.ShapeDtypeStruct(total.shape, jnp.float32)
    weight = jax.ShapeDtypeStruct(mine.shape, jnp.float32)
    work = sum(bank.shape[0] * bank.shape[1] for bank in banks) * len(shares) // SHARES
    banks = [pltpu.with_memory_space_constraint(bank, pltpu.VMEM) for bank in banks]
    args = [*pieces, *earlier, *banks, *([] if first else [before])]
    blocks = pairs // min(COLUMNS, pairs)
    return pl.pallas_call(
        functools.partial(potential_kernel, shares, pack, first, last, scale),
        out_shape=(out, weight) if last else total,
        in_specs=[VMEM] * len(args),
        out_specs=(HBM, HBM) if last else VMEM,
        scratch_shapes=[total, mine, pltpu.SemaphoreType.DMA((blocks + 1,))] if last else [],
        compiler_params=params(),
        cost_estimate=pl.CostEstimate(
            flops=2 * work * pairs * walkers, bytes_accessed=2 * work * pairs, transcendentals=0
        ),
    )(*args)


def swap(block, bit, n):
    return lax.ppermute(block, "chol", [(i, i ^ bit) for i in range(n)])


def send(block, bit, n):
    return swap(block.astype(WIRE), bit, n).astype(jnp.float32)


ROUNDS = ((0,), (1, 4, 2), (5, 3, 6), (7,))


def per_device(green_rows, factors, noise_draws):
    walkers = green_rows.shape[0]
    vectors, pairs = factors.shape
    n = lax.axis_size("chol")
    own = vectors // n
    pack = max(1, LANES // walkers)
    scale = 1.0 / math.sqrt(vectors)
    slabs = factors.reshape(n, own, pairs)
    bands = bands_of(own)
    low_bits = [1 << b for b in range(SHARES.bit_length() - 1)]
    high_bits = [1 << b for b in range(SHARES.bit_length() - 1, n.bit_length() - 1)]

    forces, sent, noise, *banks = forces_call(green_rows, noise_draws, slabs, bands, pack)
    received = send(sent, low_bits[0], n)
    for bit in low_bits[1:]:
        part = (forces.shape[0] // 2, *forces.shape[1:])
        forces, sent = small_call(split_kernel, [part, part], forces, received)
        received = send(sent, bit, n)
    forces, received = forces[0], received[0]
    for i, bit in enumerate(high_bits):
        other = swap(noise, high_bits[-1 - i], n)
        (noise,) = small_call(join_kernel, [(2 * noise.shape[0], *noise.shape[1:])], noise, other)
        (forces,) = small_call(add_kernel, [forces.shape], forces, received)
        received = send(forces, bit, n)

    pieces = {0: fields_call(forces, received, noise)}
    for share, source, bit in ((4, 0, 4), (2, 0, 2), (1, 0, 1), (6, 4, 2), (5, 4, 1), (3, 2, 1), (7, 6, 1)):
        pieces[share] = swap(pieces[source], bit, n)
    potential, used = None, ()
    for i, shares in enumerate(ROUNDS):
        here = tuple(pieces[share] for share in shares)
        earlier = used if i == len(ROUNDS) - 1 else ()
        potential = potential_call(shares, here, earlier, banks, potential, walkers, pack, scale)
        used += here
    potential, weight = potential
    return (potential, weight.reshape(-1))


def solution(mesh):
    return jax.shard_map(
        per_device,
        mesh=mesh,
        in_specs=(P("groups", "chol"), P(None, "chol"), P("groups", "chol")),
        out_specs=(P("groups", "chol"), P(("groups", "chol"))),
        check_vma=False,
    )
```

time: 173 us -> 53.8 us (0.31)
  waiting for transfers between devices: 65.8 us -> 12.1 us
  blocking collectives: 51.2 us -> 0 us
  matrix products: 36.1 us -> 0 us
  Pallas kernels: 0 us -> 26.1 us
  starting transfers between devices: 0.04 us -> 14.5 us
  between operations: 14.7 us -> 0.77 us
  local copies, waits for them, and re-layouts: 4.26 us -> 0 us
    unnamed x2 -> x0, waiting for transfers between devices: 65.8 us -> none
    unnamed x1 -> x0, blocking collectives: 29.8 us -> none
    pallas_call x0 -> x10, Pallas kernels: none -> 26.1 us  [the longest x1 16.7 us: forces_call(): pl.pallas_call(functools.partial(forces_kernel, bands, pack), out_shape=(...]
    all_gather x1 -> x0, blocking collectives: 21.4 us -> none  [per_device(): lax.all_gather(field_low, 'chol', axis=1, tiled=True)]
    unnamed x1 -> x0, matrix products: 18.5 us -> none
    dot_general x1 -> x0, matrix products: 17.7 us -> none  [per_device(): jnp.dot(lax.all_gather(field_low, 'chol', axis=1, tiled=True), factors, p...]
    ppermute x0 -> x12, starting transfers between devices: none -> 14.5 us  [swap(): return lax.ppermute(block, 'chol', [(i, i ^ bit) for i in range(n)])]
    ppermute x0 -> x12, waiting for transfers between devices: none -> 12.1 us  [swap(): return lax.ppermute(block, 'chol', [(i, i ^ bit) for i in range(n)])]
  transfers between devices with their start and end apart: 1 -> 12, of which waited for: 1 -> 6; matrix products, arithmetic and copies ran while one was open for 0% -> 0% of each run, Pallas kernels for 0% -> 14%
where the time goes in v2:
time: 53.8 us; the launch traced here: 53.7 us
  Pallas kernels  26.1 us (49%)
  starting transfers between devices  14.5 us (27%)
  waiting for transfers between devices  12.1 us (22%)
  between operations  0.77 us (1%)
    pallas_call x1, Pallas kernels, forces_call(): pl.pallas_call(functools.partial(forces_kernel, bands, pack), out_shape=(...  16.7 us
    ppermute x12, starting transfers between devices, swap(): return lax.ppermute(block, 'chol', [(i, i ^ bit) for i in range(n)])  14.5 us
    ppermute x12, waiting for transfers between devices, swap(): return lax.ppermute(block, 'chol', [(i, i ^ bit) for i in range(n)])  12.1 us
    pallas_call x4, Pallas kernels, potential_call(): pl.pallas_call(functools.partial(potential_kernel, shares, pack, first, l...  9.25 us
  transfers between devices with their start and end apart: 12, of which 6 were waited for; matrix products, arithmetic and copies ran while one was open for 0% of the time, Pallas kernels for 14%

profile of v2, /device:TPU:0, one launch (start us, length us, event | category | flops | bytes accessed | tf_op | source)
XLA Modules:
  0.0 53.7 jit_solution(6841069808826913140)
XLA Ops:
  0.6 16.7 %shard_map.50 = (f32[4,2,160,128]{3,2,1,0:T(8,128)S(1)}, f32[4,2,160,128]{3,2,1,0:T(8,128)S(1)}, f32[1,160,128]{2,1,0:T(8,128)S(1)}, bf16[16,80,4096]{2,1,0:T(8,...) custom-call(bf16[64,4096]{1,0:T(8,128)(2,1)} %rows_hbm.1, ...), custom_call_target="tpu_custom_call" | custom-call | flops 2684354560 | bytes 41943040 | tf_op jit(solution)/shard_map/pallas_call | solution.py:100
  17.4 0.6 %collective-permute-start = (f16[4,2,160,128]{3,2,1,0:T(8,128)(2,1)S(1)}, f16[4,2,160,128]{3,2,1,0:T(8,128)(2,1)S(1)}, u32[]{:S(2)}, u32[]{:S(2)}) collective-permute-start(f16[4,2,160,128]{3,2,1,0:T(8,128)(2,1)S(1)} %convert_element_type.22), channel_id=1, source_target_pairs={{0,1},{1,0},{2,3},{3,2},{4,5},{5,4},{6,7},{7,6},{8,9},{9,8},{10,11... | collective-permute-start | bytes 983048 | tf_op jit(solution)/shard_map/ppermute | solution.py:266
  17.9 1.3 %collective-permute-done = f16[4,2,160,128]{3,2,1,0:T(8,128)(2,1)S(1)} collective-permute-done((f16[4,2,160,128]{3,2,1,0:T(8,128)(2,1)S(1)}, f16[4,2,160,128]{3,2,1,0:T(8,128)(2,1)S(1)}, u32[]{:S(2)}, u32[]{:S(2)}) %collective-permute-start) | collective-permute-done | bytes 327712 | tf_op jit(solution)/shard_map/ppermute | solution.py:266
  19.2 0.1 shard_map.51
  19.4 2.9 %collective-permute-start.1 = (f16[2,2,160,128]{3,2,1,0:T(8,128)(2,1)S(1)}, f16[2,2,160,128]{3,2,1,0:T(8,128)(2,1)S(1)}, u32[]{:S(2)}, u32[]{:S(2)}) collective-permute-start(f16[2,2,160,128]{3,2,1,0:T(8,128)(2,1)S(1)} %convert_element_type.24), channel_id=1, source_target_pairs={{0,2},{1,3},{2,0},{3,1},{4,6},{5,7},{6,4},{7,5},{8,10},{9,11},{10,... | collective-permute-start | bytes 491528 | tf_op jit(solution)/shard_map/ppermute | solution.py:266
  22.3 4.5 %collective-permute-done.1 = f16[2,2,160,128]{3,2,1,0:T(8,128)(2,1)S(1)} collective-permute-done((f16[2,2,160,128]{3,2,1,0:T(8,128)(2,1)S(1)}, f16[2,2,160,128]{3,2,1,0:T(8,128)(2,1)S(1)}, u32[]{:S(2)}, u32[]{:S(2)}) %collective-permute-start.1) | collective-permute-done | bytes 163872 | tf_op jit(solution)/shard_map/ppermute | solution.py:266
  26.9 1.9 %collective-permute-start.2 = (f16[1,2,160,128]{3,2,1,0:T(8,128)(2,1)S(1)}, f16[1,2,160,128]{3,2,1,0:T(8,128)(2,1)S(1)}, u32[]{:S(2)}, u32[]{:S(2)}) collective-permute-start(f16[1,2,160,128]{3,2,1,0:T(8,128)(2,1)S(1)} %convert_element_type.26), channel_id=1, source_target_pairs={{0,4},{1,5},{2,6},{3,7},{4,0},{5,1},{6,2},{7,3},{8,12},{9,13},{10,... | collective-permute-start | bytes 245768 | tf_op jit(solution)/shard_map/ppermute | solution.py:266
  28.7 2.6 %collective-permute-start.4 = (f32[1,160,128]{2,1,0:T(8,128)S(1)}, f32[1,160,128]{2,1,0:T(8,128)S(1)}, u32[]{:S(2)}, u32[]{:S(2)}) collective-permute-start(f32[1,160,128]{2,1,0:T(8,128)S(1)} %get-tuple-element.21.first), channel_id=1, source_target_pairs={{0,8},{1,9},{2,10},{3,11},{4,12},{5,13},{6,14},{7,15},{8,0},{9,1},... | collective-permute-start | bytes 245768 | tf_op jit(solution)/shard_map/ppermute | solution.py:266
  31.3 0.9 %collective-permute-done.2 = f16[1,2,160,128]{3,2,1,0:T(8,128)(2,1)S(1)} collective-permute-done((f16[1,2,160,128]{3,2,1,0:T(8,128)(2,1)S(1)}, f16[1,2,160,128]{3,2,1,0:T(8,128)(2,1)S(1)}, u32[]{:S(2)}, u32[]{:S(2)}) %collective-permute-start.2) | collective-permute-done | bytes 81952 | tf_op jit(solution)/shard_map/ppermute | solution.py:266
  32.3 2.1 %collective-permute-start.3 = (f16[2,160,128]{2,1,0:T(8,128)(2,1)S(1)}, f16[2,160,128]{2,1,0:T(8,128)(2,1)S(1)}, u32[]{:S(2)}, u32[]{:S(2)}) collective-permute-start(f16[2,160,128]{2,1,0:T(8,128)(2,1)S(1)} %convert_element_type.27), channel_id=1, source_target_pairs={{0,8},{1,9},{2,10},{3,11},{4,12},{5,13},{6,14},{7,15},{8,0},{9,1},... | collective-permute-start | bytes 245768 | tf_op jit(solution)/shard_map/ppermute | solution.py:266
  34.4 1.8 %collective-permute-done.4.second = f32[1,160,128]{2,1,0:T(8,128)S(1)} collective-permute-done((f32[1,160,128]{2,1,0:T(8,128)S(1)}, f32[1,160,128]{2,1,0:T(8,128)S(1)}, u32[]{:S(2)}, u32[]{:S(2)}) %collective-permute-start.4) | collective-permute-done | bytes 81952 | tf_op jit(solution)/shard_map/ppermute | solution.py:266
  36.2 2.3 %collective-permute-done.3 = f16[2,160,128]{2,1,0:T(8,128)(2,1)S(1)} collective-permute-done((f16[2,160,128]{2,1,0:T(8,128)(2,1)S(1)}, f16[2,160,128]{2,1,0:T(8,128)(2,1)S(1)}, u32[]{:S(2)}, u32[]{:S(2)}) %collective-permute-start.3) | collective-permute-done | bytes 81952 | tf_op jit(solution)/shard_map/ppermute | solution.py:266
  38.6 0.1 shard_map.55.refs_0_.refs_1_
  38.6 0.5 collective-permute-start.5
  39.2 1.5 %collective-permute-start.9 = (bf16[336,128]{1,0:T(8,128)(2,1)S(1)}, bf16[336,128]{1,0:T(8,128)(2,1)S(1)}, u32[]{:S(2)}, u32[]{:S(2)}) collective-permute-start(bf16[336,128]{1,0:T(8,128)(2,1)S(1)} %shard_map.55.refs_0_.refs_1_), channel_id=1, source_target_pairs={{0,2},{1,3},{2,0},{3,1},{4,6},{5,7},{6,4},{7,5},{8,10},{9,11},{10,... | collective-permute-start | bytes 258056 | tf_op jit(solution)/shard_map/ppermute | solution.py:266
  40.7 1.1 %shard_map.56.refs_7_ = f32[64,4096]{1,0:T(8,128)S(1)} custom-call(bf16[336,128]{1,0:T(8,128)(2,1)S(1)} %shard_map.55.refs_0_.refs_1_, bf16[16,80,4096]{2,1,0:T(8,128)(2,1)S(1)} %get-tuple-element.22.refs_1_.refs_3_.refs_8_, bf16[16,80,4096]{2,1,0:T(8,128)(2,1)S(1)} %get-tuple-element.23.refs_2_.refs_4_.refs_9_, ...), custom_call_target="tpu_custom_call" | custom-call | flops 335544320 | bytes 5242880 | tf_op jit(solution)/shard_map/pallas_call | solution.py:252
  41.8 1.3 %collective-permute-done.5.refs_1_.refs_3_ = bf16[336,128]{1,0:T(8,128)(2,1)S(1)} collective-permute-done((bf16[336,128]{1,0:T(8,128)(2,1)S(1)}, bf16[336,128]{1,0:T(8,128)(2,1)S(1)}, u32[]{:S(2)}, u32[]{:S(2)}) %collective-permute-start.5) | collective-permute-done | bytes 86048 | tf_op jit(solution)/shard_map/ppermute | solution.py:266
  43.2 0.0 collective-permute-start.10
  43.2 1.7 %collective-permute-start.6 = (bf16[336,128]{1,0:T(8,128)(2,1)S(1)}, bf16[336,128]{1,0:T(8,128)(2,1)S(1)}, u32[]{:S(2)}, u32[]{:S(2)}) collective-permute-start(bf16[336,128]{1,0:T(8,128)(2,1)S(1)} %collective-permute-done.5.refs_1_.refs_3_), channel_id=1, source_target_pairs={{0,2},{1,3},{2,0},{3,1},{4,6},{5,7},{6,4},{7,5},{8,10},{9,11},{10,... | collective-permute-start | bytes 258056 | tf_op jit(solution)/shard_map/ppermute | solution.py:266
  44.9 0.2 collective-permute-start.11
  45.2 3.1 %shard_map.57.refs_7_ = f32[64,4096]{1,0:T(8,128)S(1)} custom-call(bf16[336,128]{1,0:T(8,128)(2,1)S(1)} %collective-permute-done.8.refs_0_.refs_2_, bf16[336,128]{1,0:T(8,128)(2,1)S(1)} %collective-permute-done.5.refs_1_.refs_3_, bf16[336,128]{1,0:T(8,128)(2,1)S(1)} %collective-permute-done.9.refs_2_.refs_4_, ...), custom_call_target="tpu_custom_call" | custom-call | flops 1006632960 | bytes 15728640 | tf_op jit(solution)/shard_map/pallas_call | solution.py:252
  48.3 0.3 collective-permute-start.7
  48.6 3.1 %shard_map.58.refs_12_ = f32[64,4096]{1,0:T(8,128)S(1)} custom-call(bf16[336,128]{1,0:T(8,128)(2,1)S(1)} %collective-permute-done.10.refs_0_.refs_5_, bf16[336,128]{1,0:T(8,128)(2,1)S(1)} %collective-permute-done.11.refs_1_.refs_6_, bf16[336,128]{1,0:T(8,128)(2,1)S(1)} %collective-permute-done.6.refs_2_.refs_7_, ...), custom_call_target="tpu_custom_call" | custom-call | flops 1006632960 | bytes 15728640 | tf_op jit(solution)/shard_map/pallas_call | solution.py:252
  51.8 1.9 %shard_map.59 = (f32[64,4096]{1,0:T(8,128)}, f32[1,4]{1,0:T(1,128)}) custom-call(bf16[336,128]{1,0:T(8,128)(2,1)S(1)} %collective-permute-done.7.refs_0_, bf16[336,128]{1,0:T(8,128)(2,1)S(1)} %shard_map.55.refs_0_.refs_1_, bf16[336,128]{1,0:T(8,128)(2,1)S(1)} %collective-permute-done.8.refs_0_.refs_2_, ...), custom_call_target="tpu_custom_call" | custom-call | flops 335544320 | bytes 5242880 | tf_op jit(solution)/shard_map/pallas_call | solution.py:252
  (18 shorter events, 0.3 us)
Async XLA Ops:
  17.4 1.8 %collective-permute-start = (f16[4,2,160,128]{3,2,1,0:T(8,128)(2,1)S(1)}, f16[4,2,160,128]{3,2,1,0:T(8,128)(2,1)S(1)}, u32[]{:S(2)}, u32[]{:S(2)}) collective-permute-start(f16[4,2,160,128]{3,2,1,0:T(8,128)(2,1)S(1)} %convert_element_type.22), channel_id=1, source_target_pairs={{0,1},{1,0},{2,3},{3,2},{4,5},{5,4},{6,7},{7,6},{8,9},{9,8},{10,11... | collective-permute-start | bytes 983048 | tf_op jit(solution)/shard_map/ppermute | solution.py:266
  19.4 7.4 %collective-permute-start.1 = (f16[2,2,160,128]{3,2,1,0:T(8,128)(2,1)S(1)}, f16[2,2,160,128]{3,2,1,0:T(8,128)(2,1)S(1)}, u32[]{:S(2)}, u32[]{:S(2)}) collective-permute-start(f16[2,2,160,128]{3,2,1,0:T(8,128)(2,1)S(1)} %convert_element_type.24), channel_id=1, source_target_pairs={{0,2},{1,3},{2,0},{3,1},{4,6},{5,7},{6,4},{7,5},{8,10},{9,11},{10,... | collective-permute-start | bytes 491528 | tf_op jit(solution)/shard_map/ppermute | solution.py:266
  26.9 5.3 %collective-permute-start.2 = (f16[1,2,160,128]{3,2,1,0:T(8,128)(2,1)S(1)}, f16[1,2,160,128]{3,2,1,0:T(8,128)(2,1)S(1)}, u32[]{:S(2)}, u32[]{:S(2)}) collective-permute-start(f16[1,2,160,128]{3,2,1,0:T(8,128)(2,1)S(1)} %convert_element_type.26), channel_id=1, source_target_pairs={{0,4},{1,5},{2,6},{3,7},{4,0},{5,1},{6,2},{7,3},{8,12},{9,13},{10,... | collective-permute-start | bytes 245768 | tf_op jit(solution)/shard_map/ppermute | solution.py:266
  28.7 7.5 %collective-permute-start.4 = (f32[1,160,128]{2,1,0:T(8,128)S(1)}, f32[1,160,128]{2,1,0:T(8,128)S(1)}, u32[]{:S(2)}, u32[]{:S(2)}) collective-permute-start(f32[1,160,128]{2,1,0:T(8,128)S(1)} %get-tuple-element.21.first), channel_id=1, source_target_pairs={{0,8},{1,9},{2,10},{3,11},{4,12},{5,13},{6,14},{7,15},{8,0},{9,1},... | collective-permute-start | bytes 245768 | tf_op jit(solution)/shard_map/ppermute | solution.py:266
  32.3 6.3 %collective-permute-start.3 = (f16[2,160,128]{2,1,0:T(8,128)(2,1)S(1)}, f16[2,160,128]{2,1,0:T(8,128)(2,1)S(1)}, u32[]{:S(2)}, u32[]{:S(2)}) collective-permute-start(f16[2,160,128]{2,1,0:T(8,128)(2,1)S(1)} %convert_element_type.27), channel_id=1, source_target_pairs={{0,8},{1,9},{2,10},{3,11},{4,12},{5,13},{6,14},{7,15},{8,0},{9,1},... | collective-permute-start | bytes 245768 | tf_op jit(solution)/shard_map/ppermute | solution.py:266
  38.6 4.5 %collective-permute-start.5 = (bf16[336,128]{1,0:T(8,128)(2,1)S(1)}, bf16[336,128]{1,0:T(8,128)(2,1)S(1)}, u32[]{:S(2)}, u32[]{:S(2)}) collective-permute-start(bf16[336,128]{1,0:T(8,128)(2,1)S(1)} %shard_map.55.refs_0_.refs_1_), channel_id=1, source_target_pairs={{0,4},{1,5},{2,6},{3,7},{4,0},{5,1},{6,2},{7,3},{8,12},{9,13},{10,... | collective-permute-start | bytes 258056 | tf_op jit(solution)/shard_map/ppermute | solution.py:266
  39.2 5.8 %collective-permute-start.9 = (bf16[336,128]{1,0:T(8,128)(2,1)S(1)}, bf16[336,128]{1,0:T(8,128)(2,1)S(1)}, u32[]{:S(2)}, u32[]{:S(2)}) collective-permute-start(bf16[336,128]{1,0:T(8,128)(2,1)S(1)} %shard_map.55.refs_0_.refs_1_), channel_id=1, source_target_pairs={{0,2},{1,3},{2,0},{3,1},{4,6},{5,7},{6,4},{7,5},{8,10},{9,11},{10,... | collective-permute-start | bytes 258056 | tf_op jit(solution)/shard_map/ppermute | solution.py:266
  40.7 4.5 %collective-permute-start.8 = (bf16[336,128]{1,0:T(8,128)(2,1)S(1)}, bf16[336,128]{1,0:T(8,128)(2,1)S(1)}, u32[]{:S(2)}, u32[]{:S(2)}) collective-permute-start(bf16[336,128]{1,0:T(8,128)(2,1)S(1)} %shard_map.55.refs_0_.refs_1_), channel_id=1, source_target_pairs={{0,1},{1,0},{2,3},{3,2},{4,5},{5,4},{6,7},{7,6},{8,9},{9,8},{10,11... | collective-permute-start | bytes 258056 | tf_op jit(solution)/shard_map/ppermute | solution.py:266
  43.2 5.5 %collective-permute-start.10 = (bf16[336,128]{1,0:T(8,128)(2,1)S(1)}, bf16[336,128]{1,0:T(8,128)(2,1)S(1)}, u32[]{:S(2)}, u32[]{:S(2)}) collective-permute-start(bf16[336,128]{1,0:T(8,128)(2,1)S(1)} %collective-permute-done.5.refs_1_.refs_3_), channel_id=1, source_target_pairs={{0,1},{1,0},{2,3},{3,2},{4,5},{5,4},{6,7},{7,6},{8,9},{9,8},{10,11... | collective-permute-start | bytes 258056 | tf_op jit(solution)/shard_map/ppermute | solution.py:266
  43.2 5.1 %collective-permute-start.6 = (bf16[336,128]{1,0:T(8,128)(2,1)S(1)}, bf16[336,128]{1,0:T(8,128)(2,1)S(1)}, u32[]{:S(2)}, u32[]{:S(2)}) collective-permute-start(bf16[336,128]{1,0:T(8,128)(2,1)S(1)} %collective-permute-done.5.refs_1_.refs_3_), channel_id=1, source_target_pairs={{0,2},{1,3},{2,0},{3,1},{4,6},{5,7},{6,4},{7,5},{8,10},{9,11},{10,... | collective-permute-start | bytes 258056 | tf_op jit(solution)/shard_map/ppermute | solution.py:266
  44.9 3.7 %collective-permute-start.11 = (bf16[336,128]{1,0:T(8,128)(2,1)S(1)}, bf16[336,128]{1,0:T(8,128)(2,1)S(1)}, u32[]{:S(2)}, u32[]{:S(2)}) collective-permute-start(bf16[336,128]{1,0:T(8,128)(2,1)S(1)} %collective-permute-done.9.refs_2_.refs_4_), channel_id=1, source_target_pairs={{0,1},{1,0},{2,3},{3,2},{4,5},{5,4},{6,7},{7,6},{8,9},{9,8},{10,11... | collective-permute-start | bytes 258056 | tf_op jit(solution)/shard_map/ppermute | solution.py:266
  48.3 3.5 %collective-permute-start.7 = (bf16[336,128]{1,0:T(8,128)(2,1)S(1)}, bf16[336,128]{1,0:T(8,128)(2,1)S(1)}, u32[]{:S(2)}, u32[]{:S(2)}) collective-permute-start(bf16[336,128]{1,0:T(8,128)(2,1)S(1)} %collective-permute-done.6.refs_2_.refs_7_), channel_id=1, source_target_pairs={{0,1},{1,0},{2,3},{3,2},{4,5},{5,4},{6,7},{7,6},{8,9},{9,8},{10,11... | collective-permute-start | bytes 258056 | tf_op jit(solution)/shard_map/ppermute | solution.py:266

commit v3 on v2

--- a/solution.py
+++ b/solution.py
@@ -11,6 +11,7 @@
 LANES = 128
 TILE = 16
 MARGIN = 4 * 1024 * 1024
+PRODUCT_LIMIT = 10 * 1024 * 1024
 SHARES = 8
 BANKS = 4
 COLUMNS = 1024
@@ -43,70 +44,57 @@
     return lax.rem(owner, SHARES) ^ lax.rem(me, SHARES)
 
 
-def forces_kernel(bands, pack, rows_hbm, noise_hbm, slabs, kept, sent, draws, *refs):
+def forces_kernel(bands, pack, rows_hbm, noise_hbm, slabs, halves, draws, *refs):
     *banks, rows_in, noise, sems = refs
-    n, size, _ = slabs.shape
+    n, _, _ = slabs.shape
     me = lax.axis_index("chol")
 
     def fetch(d, b):
         lo, hi = bands[b]
         return pltpu.make_async_copy(slabs.at[d, lo:hi], banks[b].at[d], sems.at[d * BANKS + b])
 
+    noise_copy = pltpu.make_async_copy(noise_hbm, noise, sems.at[n * BANKS + 1])
+    noise_copy.start()
     rows_copy = pltpu.make_async_copy(rows_hbm, rows_in, sems.at[n * BANKS])
     rows_copy.start()
     for d in range(n):
         for b in range(BANKS):
             fetch(d, b).start()
-    noise_copy = pltpu.make_async_copy(noise_hbm, noise, sems.at[n * BANKS + 1])
-    noise_copy.start()
+    noise_copy.wait()
+    draws[0] = pack_rows(noise[...].T, pack)
     rows_copy.wait()
 
     def step(group, i, _):
-        parts = []
         for j in range(group):
             for b in range(BANKS):
                 fetch(i * group + j, b).wait()
         for j in range(group):
-            parts += [bank[i * group + j] for bank in banks]
-        part = lax.dot_general(
-            jnp.concatenate(parts, axis=0),
-            rows_in[...],
-            (((1,), (1,)), ((), ())),
-            preferred_element_type=jnp.float32,
-        )
-        for j in range(group):
             owner = i * group + j
+            part = lax.dot_general(
+                jnp.concatenate([bank[owner] for bank in banks], axis=0),
+                rows_in[...],
+                (((1,), (1,)), ((), ())),
+                preferred_element_type=jnp.float32,
+            )
             share = share_of(owner, me)
-            packed = pack_rows(part[j * size : (j + 1) * size], pack)
-
-            @pl.when(share % 2 == 0)
-            def _():
-                kept[share // 2, owner // SHARES] = packed
-
-            @pl.when(share % 2 == 1)
-            def _():
-                sent[share // 2, owner // SHARES] = packed
-
-    lax.fori_loop(0, n // 2 - 1, functools.partial(step, 2), None)
-    lax.fori_loop(n - 2, n, functools.partial(step, 1), None)
-    noise_copy.wait()
-    draws[0] = pack_rows(noise[...].T, pack)
+            halves[share % 2, share // 2, owner // SHARES] = pack_rows(part, pack)
+
+    lax.fori_loop(0, n // 2, functools.partial(step, 2), None)
 
 
 def forces_call(rows_in, noise, slabs, bands, pack):
     walkers, pairs = rows_in.shape
     n, size, _ = slabs.shape
-    half = (SHARES // 2, n // SHARES, size // pack, walkers * pack)
+    halves = (2, SHARES // 2, n // SHARES, size // pack, walkers * pack)
     return pl.pallas_call(
         functools.partial(forces_kernel, bands, pack),
         out_shape=(
-            pltpu.VMEM(half, jnp.float32),
-            pltpu.VMEM(half, jnp.float32),
-            pltpu.VMEM((1, *half[2:]), jnp.float32),
+            pltpu.VMEM(halves, jnp.float32),
+            pltpu.VMEM((1, *halves[3:]), jnp.float32),
             *[pltpu.VMEM((n, hi - lo, pairs), jnp.bfloat16) for lo, hi in bands],
         ),
         in_specs=[HBM, HBM, HBM],
-        out_specs=(VMEM,) * (3 + BANKS),
+        out_specs=(VMEM,) * (2 + BANKS),
         scratch_shapes=[
             pltpu.VMEM(rows_in.shape, rows_in.dtype),
             pltpu.VMEM(noise.shape, noise.dtype),
@@ -129,10 +117,17 @@
     )(*args)
 
 
-def split_kernel(kept, received, out, sent):
-    for i in range(out.shape[0]):
-        out[i] = kept[2 * i] + received[2 * i]
-        sent[i] = kept[2 * i + 1] + received[2 * i + 1]
+def spread_kernel(halves, received, *outs):
+    for k, out in enumerate(outs):
+        out[...] = halves[0, k] + received[k]
+
+
+def sum_kernel(kept, *refs):
+    *received, out = refs
+    total = kept[...]
+    for ref in received:
+        total += ref[...]
+    out[...] = total
 
 
 def add_kernel(kept, received, out):
@@ -255,7 +250,7 @@
         in_specs=[VMEM] * len(args),
         out_specs=(HBM, HBM) if last else VMEM,
         scratch_shapes=[total, mine, pltpu.SemaphoreType.DMA((blocks + 1,))] if last else [],
-        compiler_params=params(),
+        compiler_params=params(PRODUCT_LIMIT),
         cost_estimate=pl.CostEstimate(
             flops=2 * work * pairs * walkers, bytes_accessed=2 * work * pairs, transcendentals=0
         ),
@@ -270,7 +265,7 @@
     return swap(block.astype(WIRE), bit, n).astype(jnp.float32)
 
 
-ROUNDS = ((0,), (1, 4, 2), (5, 3, 6), (7,))
+ROUNDS = ((0, 1), (4, 2, 5, 3), (6,), (7,))
 
 
 def per_device(green_rows, factors, noise_draws):
@@ -282,20 +277,20 @@
     scale = 1.0 / math.sqrt(vectors)
     slabs = factors.reshape(n, own, pairs)
     bands = bands_of(own)
-    low_bits = [1 << b for b in range(SHARES.bit_length() - 1)]
     high_bits = [1 << b for b in range(SHARES.bit_length() - 1, n.bit_length() - 1)]
 
-    forces, sent, noise, *banks = forces_call(green_rows, noise_draws, slabs, bands, pack)
-    received = send(sent, low_bits[0], n)
-    for bit in low_bits[1:]:
-        part = (forces.shape[0] // 2, *forces.shape[1:])
-        forces, sent = small_call(split_kernel, [part, part], forces, received)
-        received = send(sent, bit, n)
-    forces, received = forces[0], received[0]
+    halves, noise, *banks = forces_call(green_rows, noise_draws, slabs, bands, pack)
+    received = send(halves[1], 1, n)
+    part = halves.shape[2:]
+    forces, *sent = small_call(spread_kernel, [part] * (SHARES // 2), halves, received)
+    arrived = [send(block, 2 * k + 2, n) for k, block in enumerate(sent)]
+    (forces,) = small_call(sum_kernel, [part], forces, *arrived)
+    received = None
     for i, bit in enumerate(high_bits):
         other = swap(noise, high_bits[-1 - i], n)
         (noise,) = small_call(join_kernel, [(2 * noise.shape[0], *noise.shape[1:])], noise, other)
-        (forces,) = small_call(add_kernel, [forces.shape], forces, received)
+        if received is not None:
+            (forces,) = small_call(add_kernel, [part], forces, received)
         received = send(forces, bit, n)
 
     pieces = {0: fields_call(forces, received, noise)}

time: 53.8 us -> 51.9 us (0.965)
  starting transfers between devices: 14.5 us -> 11.5 us
  waiting for transfers between devices: 12.1 us -> 13.8 us
  Pallas kernels: 26.1 us -> 25.4 us
    ppermute x12 -> x13, starting transfers between devices: 14.5 us -> 11.5 us  [swap(): return lax.ppermute(block, 'chol', [(i, i ^ bit) for i in range(n)])]
    ppermute x12 -> x13, waiting for transfers between devices: 12.1 us -> 13.8 us  [swap(): return lax.ppermute(block, 'chol', [(i, i ^ bit) for i in range(n)])]
    pallas_call x1, Pallas kernels: 16.7 us -> 16 us  [forces_call(): pl.pallas_call(functools.partial(forces_kernel, bands, pack), out_shape=(...]
  transfers between devices with their start and end apart: 12 -> 13, of which waited for: 6 -> 6; matrix products, arithmetic and copies ran while one was open for 0% -> 0% of each run, Pallas kernels for 14% -> 14%
where the time goes in v3:
time: 51.9 us; the launch traced here: 51.7 us
  Pallas kernels  25.4 us (49%)
  waiting for transfers between devices  13.8 us (27%)
  starting transfers between devices  11.5 us (22%)
  between operations  0.78 us (2%)
    pallas_call x1, Pallas kernels, forces_call(): pl.pallas_call(functools.partial(forces_kernel, bands, pack), out_shape=(...  16 us
    ppermute x13, waiting for transfers between devices, swap(): return lax.ppermute(block, 'chol', [(i, i ^ bit) for i in range(n)])  13.8 us
    ppermute x13, starting transfers between devices, swap(): return lax.ppermute(block, 'chol', [(i, i ^ bit) for i in range(n)])  11.5 us
    pallas_call x4, Pallas kernels, potential_call(): pl.pallas_call(functools.partial(potential_kernel, shares, pack, first, l...  9.21 us
  transfers between devices with their start and end apart: 13, of which 6 were waited for; matrix products, arithmetic and copies ran while one was open for 0% of the time, Pallas kernels for 14%

profile of v3, /device:TPU:0, one launch (start us, length us, event | category | flops | bytes accessed | tf_op | source)
XLA Modules:
  0.0 51.7 jit_solution(18191797841600143096)
XLA Ops:
  0.6 16.0 %shard_map.50 = (f32[2,4,2,160,128]{4,3,2,1,0:T(8,128)S(1)}, f32[1,160,128]{2,1,0:T(8,128)S(1)}, bf16[16,80,4096]{2,1,0:T(8,128)(2,1)S(1)}, bf16[16,80,4096]{2,1...) custom-call(bf16[64,4096]{1,0:T(8,128)(2,1)} %rows_hbm.1, ...), custom_call_target="tpu_custom_call" | custom-call | flops 2684354560 | bytes 41943040 | tf_op jit(solution)/shard_map/pallas_call | solution.py:89
  16.7 0.6 %collective-permute-start = (f16[4,2,160,128]{3,2,1,0:T(8,128)(2,1)S(1)}, f16[4,2,160,128]{3,2,1,0:T(8,128)(2,1)S(1)}, u32[]{:S(2)}, u32[]{:S(2)}) collective-permute-start(f16[4,2,160,128]{3,2,1,0:T(8,128)(2,1)S(1)} %fusion), channel_id=1, source_target_pairs={{0,1},{1,0},{2,3},{3,2},{4,5},{5,4},{6,7},{7,6},{8,9},{9,8},{10,11... | collective-permute-start | bytes 983048 | tf_op jit(solution)/shard_map/ppermute | solution.py:261
  17.2 1.3 %collective-permute-done = f16[4,2,160,128]{3,2,1,0:T(8,128)(2,1)S(1)} collective-permute-done((f16[4,2,160,128]{3,2,1,0:T(8,128)(2,1)S(1)}, f16[4,2,160,128]{3,2,1,0:T(8,128)(2,1)S(1)}, u32[]{:S(2)}, u32[]{:S(2)}) %collective-permute-start) | collective-permute-done | bytes 327712 | tf_op jit(solution)/shard_map/ppermute | solution.py:261
  18.6 0.1 shard_map.51
  18.7 4.0 %collective-permute-start.3 = (f16[2,160,128]{2,1,0:T(8,128)(2,1)S(1)}, f16[2,160,128]{2,1,0:T(8,128)(2,1)S(1)}, u32[]{:S(2)}, u32[]{:S(2)}) collective-permute-start(f16[2,160,128]{2,1,0:T(8,128)(2,1)S(1)} %convert_element_type.37), channel_id=1, source_target_pairs={{0,6},{1,7},{2,4},{3,5},{4,2},{5,3},{6,0},{7,1},{8,14},{9,15},{10,... | collective-permute-start | bytes 245768 | tf_op jit(solution)/shard_map/ppermute | solution.py:261
  22.6 0.5 collective-permute-start.2
  23.1 0.2 collective-permute-start.1
  23.4 2.9 %collective-permute-start.5 = (f32[1,160,128]{2,1,0:T(8,128)S(1)}, f32[1,160,128]{2,1,0:T(8,128)S(1)}, u32[]{:S(2)}, u32[]{:S(2)}) collective-permute-start(f32[1,160,128]{2,1,0:T(8,128)S(1)} %get-tuple-element.19.first), channel_id=1, source_target_pairs={{0,8},{1,9},{2,10},{3,11},{4,12},{5,13},{6,14},{7,15},{8,0},{9,1},... | collective-permute-start | bytes 245768 | tf_op jit(solution)/shard_map/ppermute | solution.py:261
  26.3 2.8 %collective-permute-done.2 = f16[2,160,128]{2,1,0:T(8,128)(2,1)S(1)} collective-permute-done((f16[2,160,128]{2,1,0:T(8,128)(2,1)S(1)}, f16[2,160,128]{2,1,0:T(8,128)(2,1)S(1)}, u32[]{:S(2)}, u32[]{:S(2)}) %collective-permute-start.2) | collective-permute-done | bytes 81952 | tf_op jit(solution)/shard_map/ppermute | solution.py:261
  29.1 0.0 collective-permute-done.1
  29.2 1.5 %collective-permute-start.4 = (f16[2,160,128]{2,1,0:T(8,128)(2,1)S(1)}, f16[2,160,128]{2,1,0:T(8,128)(2,1)S(1)}, u32[]{:S(2)}, u32[]{:S(2)}) collective-permute-start(f16[2,160,128]{2,1,0:T(8,128)(2,1)S(1)} %convert_element_type.39), channel_id=1, source_target_pairs={{0,8},{1,9},{2,10},{3,11},{4,12},{5,13},{6,14},{7,15},{8,0},{9,1},... | collective-permute-start | bytes 245768 | tf_op jit(solution)/shard_map/ppermute | solution.py:261
  30.7 4.7 %collective-permute-done.4 = f16[2,160,128]{2,1,0:T(8,128)(2,1)S(1)} collective-permute-done((f16[2,160,128]{2,1,0:T(8,128)(2,1)S(1)}, f16[2,160,128]{2,1,0:T(8,128)(2,1)S(1)}, u32[]{:S(2)}, u32[]{:S(2)}) %collective-permute-start.4) | collective-permute-done | bytes 81952 | tf_op jit(solution)/shard_map/ppermute | solution.py:261
  35.4 0.1 shard_map.54.refs_0_.refs_1_
  35.5 0.1 collective-permute-start.6
  35.6 0.8 %collective-permute-start.10 = (bf16[336,128]{1,0:T(8,128)(2,1)S(1)}, bf16[336,128]{1,0:T(8,128)(2,1)S(1)}, u32[]{:S(2)}, u32[]{:S(2)}) collective-permute-start(bf16[336,128]{1,0:T(8,128)(2,1)S(1)} %shard_map.54.refs_0_.refs_1_), channel_id=1, source_target_pairs={{0,2},{1,3},{2,0},{3,1},{4,6},{5,7},{6,4},{7,5},{8,10},{9,11},{10,... | collective-permute-start | bytes 258056 | tf_op jit(solution)/shard_map/ppermute | solution.py:261
  36.4 3.6 %collective-permute-done.6.refs_0_.refs_3_ = bf16[336,128]{1,0:T(8,128)(2,1)S(1)} collective-permute-done((bf16[336,128]{1,0:T(8,128)(2,1)S(1)}, bf16[336,128]{1,0:T(8,128)(2,1)S(1)}, u32[]{:S(2)}, u32[]{:S(2)}) %collective-permute-start.6) | collective-permute-done | bytes 86048 | tf_op jit(solution)/shard_map/ppermute | solution.py:261
  40.1 0.4 collective-permute-start.7
  40.5 0.2 collective-permute-done.10.refs_1_.refs_4_
  40.7 0.5 collective-permute-start.11
  41.2 2.1 %shard_map.55.refs_8_ = f32[64,4096]{1,0:T(8,128)S(1)} custom-call(bf16[336,128]{1,0:T(8,128)(2,1)S(1)} %shard_map.54.refs_0_.refs_1_, bf16[336,128]{1,0:T(8,128)(2,1)S(1)} %collective-permute-done.9.refs_1_.refs_2_, bf16[16,80,4096]{2,1,0:T(8,128)(2,1)S(1)} %get-tuple-element.20.refs_2_.refs_4_.refs_1_.refs_8_, ...), custom_call_target="tpu_custom_call" | custom-call | flops 671088640 | bytes 10485760 | tf_op jit(solution)/shard_map/pallas_call | solution.py:247
  43.3 1.2 %collective-permute-done.7.refs_0_.refs_7_ = bf16[336,128]{1,0:T(8,128)(2,1)S(1)} collective-permute-done((bf16[336,128]{1,0:T(8,128)(2,1)S(1)}, bf16[336,128]{1,0:T(8,128)(2,1)S(1)}, u32[]{:S(2)}, u32[]{:S(2)}) %collective-permute-start.7) | collective-permute-done | bytes 86048 | tf_op jit(solution)/shard_map/ppermute | solution.py:261
  44.6 4.0 %shard_map.56.refs_5_ = f32[64,4096]{1,0:T(8,128)S(1)} custom-call(bf16[336,128]{1,0:T(8,128)(2,1)S(1)} %collective-permute-done.6.refs_0_.refs_3_, bf16[336,128]{1,0:T(8,128)(2,1)S(1)} %collective-permute-done.10.refs_1_.refs_4_, bf16[336,128]{1,0:T(8,128)(2,1)S(1)} %collective-permute-done.11.refs_2_.refs_5_, ...), custom_call_target="tpu_custom_call" | custom-call | flops 1342177280 | bytes 20971520 | tf_op jit(solution)/shard_map/pallas_call | solution.py:247
  48.6 1.2 %shard_map.57.refs_12_ = f32[64,4096]{1,0:T(8,128)S(1)} custom-call(bf16[336,128]{1,0:T(8,128)(2,1)S(1)} %collective-permute-done.7.refs_0_.refs_7_, bf16[16,80,4096]{2,1,0:T(8,128)(2,1)S(1)} %get-tuple-element.20.refs_2_.refs_4_.refs_1_.refs_8_, bf16[16,80,4096]{2,1,0:T(8,128)(2,1)S(1)} %get-tuple-element.21.refs_3_.refs_5_.refs_2_.refs_9_, ...), custom_call_target="tpu_custom_call" | custom-call | flops 335544320 | bytes 5242880 | tf_op jit(solution)/shard_map/pallas_call | solution.py:247
  49.8 1.9 %shard_map.58 = (f32[64,4096]{1,0:T(8,128)}, f32[1,4]{1,0:T(1,128)}) custom-call(bf16[336,128]{1,0:T(8,128)(2,1)S(1)} %collective-permute-done.8.refs_0_, bf16[336,128]{1,0:T(8,128)(2,1)S(1)} %shard_map.54.refs_0_.refs_1_, bf16[336,128]{1,0:T(8,128)(2,1)S(1)} %collective-permute-done.9.refs_1_.refs_2_, ...), custom_call_target="tpu_custom_call" | custom-call | flops 335544320 | bytes 5242880 | tf_op jit(solution)/shard_map/pallas_call | solution.py:247
  (21 shorter events, 0.3 us)
Async XLA Ops:
  16.7 1.8 %collective-permute-start = (f16[4,2,160,128]{3,2,1,0:T(8,128)(2,1)S(1)}, f16[4,2,160,128]{3,2,1,0:T(8,128)(2,1)S(1)}, u32[]{:S(2)}, u32[]{:S(2)}) collective-permute-start(f16[4,2,160,128]{3,2,1,0:T(8,128)(2,1)S(1)} %fusion), channel_id=1, source_target_pairs={{0,1},{1,0},{2,3},{3,2},{4,5},{5,4},{6,7},{7,6},{8,9},{9,8},{10,11... | collective-permute-start | bytes 983048 | tf_op jit(solution)/shard_map/ppermute | solution.py:261
  18.7 7.6 %collective-permute-start.3 = (f16[2,160,128]{2,1,0:T(8,128)(2,1)S(1)}, f16[2,160,128]{2,1,0:T(8,128)(2,1)S(1)}, u32[]{:S(2)}, u32[]{:S(2)}) collective-permute-start(f16[2,160,128]{2,1,0:T(8,128)(2,1)S(1)} %convert_element_type.37), channel_id=1, source_target_pairs={{0,6},{1,7},{2,4},{3,5},{4,2},{5,3},{6,0},{7,1},{8,14},{9,15},{10,... | collective-permute-start | bytes 245768 | tf_op jit(solution)/shard_map/ppermute | solution.py:261
  22.6 6.4 %collective-permute-start.2 = (f16[2,160,128]{2,1,0:T(8,128)(2,1)S(1)}, f16[2,160,128]{2,1,0:T(8,128)(2,1)S(1)}, u32[]{:S(2)}, u32[]{:S(2)}) collective-permute-start(f16[2,160,128]{2,1,0:T(8,128)(2,1)S(1)} %convert_element_type.35), channel_id=1, source_target_pairs={{0,4},{1,5},{2,6},{3,7},{4,0},{5,1},{6,2},{7,3},{8,12},{9,13},{10,... | collective-permute-start | bytes 245768 | tf_op jit(solution)/shard_map/ppermute | solution.py:261
  23.1 6.0 %collective-permute-start.1 = (f16[2,160,128]{2,1,0:T(8,128)(2,1)S(1)}, f16[2,160,128]{2,1,0:T(8,128)(2,1)S(1)}, u32[]{:S(2)}, u32[]{:S(2)}) collective-permute-start(f16[2,160,128]{2,1,0:T(8,128)(2,1)S(1)} %convert_element_type.33), channel_id=1, source_target_pairs={{0,2},{1,3},{2,0},{3,1},{4,6},{5,7},{6,4},{7,5},{8,10},{9,11},{10,... | collective-permute-start | bytes 245768 | tf_op jit(solution)/shard_map/ppermute | solution.py:261
  23.4 7.4 %collective-permute-start.5 = (f32[1,160,128]{2,1,0:T(8,128)S(1)}, f32[1,160,128]{2,1,0:T(8,128)S(1)}, u32[]{:S(2)}, u32[]{:S(2)}) collective-permute-start(f32[1,160,128]{2,1,0:T(8,128)S(1)} %get-tuple-element.19.first), channel_id=1, source_target_pairs={{0,8},{1,9},{2,10},{3,11},{4,12},{5,13},{6,14},{7,15},{8,0},{9,1},... | collective-permute-start | bytes 245768 | tf_op jit(solution)/shard_map/ppermute | solution.py:261
  29.2 6.2 %collective-permute-start.4 = (f16[2,160,128]{2,1,0:T(8,128)(2,1)S(1)}, f16[2,160,128]{2,1,0:T(8,128)(2,1)S(1)}, u32[]{:S(2)}, u32[]{:S(2)}) collective-permute-start(f16[2,160,128]{2,1,0:T(8,128)(2,1)S(1)} %convert_element_type.39), channel_id=1, source_target_pairs={{0,8},{1,9},{2,10},{3,11},{4,12},{5,13},{6,14},{7,15},{8,0},{9,1},... | collective-permute-start | bytes 245768 | tf_op jit(solution)/shard_map/ppermute | solution.py:261
  35.5 4.5 %collective-permute-start.6 = (bf16[336,128]{1,0:T(8,128)(2,1)S(1)}, bf16[336,128]{1,0:T(8,128)(2,1)S(1)}, u32[]{:S(2)}, u32[]{:S(2)}) collective-permute-start(bf16[336,128]{1,0:T(8,128)(2,1)S(1)} %shard_map.54.refs_0_.refs_1_), channel_id=1, source_target_pairs={{0,4},{1,5},{2,6},{3,7},{4,0},{5,1},{6,2},{7,3},{8,12},{9,13},{10,... | collective-permute-start | bytes 258056 | tf_op jit(solution)/shard_map/ppermute | solution.py:261
  35.6 5.1 %collective-permute-start.10 = (bf16[336,128]{1,0:T(8,128)(2,1)S(1)}, bf16[336,128]{1,0:T(8,128)(2,1)S(1)}, u32[]{:S(2)}, u32[]{:S(2)}) collective-permute-start(bf16[336,128]{1,0:T(8,128)(2,1)S(1)} %shard_map.54.refs_0_.refs_1_), channel_id=1, source_target_pairs={{0,2},{1,3},{2,0},{3,1},{4,6},{5,7},{6,4},{7,5},{8,10},{9,11},{10,... | collective-permute-start | bytes 258056 | tf_op jit(solution)/shard_map/ppermute | solution.py:261
  36.4 4.8 %collective-permute-start.9 = (bf16[336,128]{1,0:T(8,128)(2,1)S(1)}, bf16[336,128]{1,0:T(8,128)(2,1)S(1)}, u32[]{:S(2)}, u32[]{:S(2)}) collective-permute-start(bf16[336,128]{1,0:T(8,128)(2,1)S(1)} %shard_map.54.refs_0_.refs_1_), channel_id=1, source_target_pairs={{0,1},{1,0},{2,3},{3,2},{4,5},{5,4},{6,7},{7,6},{8,9},{9,8},{10,11... | collective-permute-start | bytes 258056 | tf_op jit(solution)/shard_map/ppermute | solution.py:261
  40.1 4.5 %collective-permute-start.7 = (bf16[336,128]{1,0:T(8,128)(2,1)S(1)}, bf16[336,128]{1,0:T(8,128)(2,1)S(1)}, u32[]{:S(2)}, u32[]{:S(2)}) collective-permute-start(bf16[336,128]{1,0:T(8,128)(2,1)S(1)} %collective-permute-done.6.refs_0_.refs_3_), channel_id=1, source_target_pairs={{0,2},{1,3},{2,0},{3,1},{4,6},{5,7},{6,4},{7,5},{8,10},{9,11},{10,... | collective-permute-start | bytes 258056 | tf_op jit(solution)/shard_map/ppermute | solution.py:261
  40.7 3.8 %collective-permute-start.12 = (bf16[336,128]{1,0:T(8,128)(2,1)S(1)}, bf16[336,128]{1,0:T(8,128)(2,1)S(1)}, u32[]{:S(2)}, u32[]{:S(2)}) collective-permute-start(bf16[336,128]{1,0:T(8,128)(2,1)S(1)} %collective-permute-done.10.refs_1_.refs_4_), channel_id=1, source_target_pairs={{0,1},{1,0},{2,3},{3,2},{4,5},{5,4},{6,7},{7,6},{8,9},{9,8},{10,11... | collective-permute-start | bytes 258056 | tf_op jit(solution)/shard_map/ppermute | solution.py:261
  40.7 3.8 %collective-permute-start.11 = (bf16[336,128]{1,0:T(8,128)(2,1)S(1)}, bf16[336,128]{1,0:T(8,128)(2,1)S(1)}, u32[]{:S(2)}, u32[]{:S(2)}) collective-permute-start(bf16[336,128]{1,0:T(8,128)(2,1)S(1)} %collective-permute-done.6.refs_0_.refs_3_), channel_id=1, source_target_pairs={{0,1},{1,0},{2,3},{3,2},{4,5},{5,4},{6,7},{7,6},{8,9},{9,8},{10,11... | collective-permute-start | bytes 258056 | tf_op jit(solution)/shard_map/ppermute | solution.py:261
  44.5 5.2 %collective-permute-start.8 = (bf16[336,128]{1,0:T(8,128)(2,1)S(1)}, bf16[336,128]{1,0:T(8,128)(2,1)S(1)}, u32[]{:S(2)}, u32[]{:S(2)}) collective-permute-start(bf16[336,128]{1,0:T(8,128)(2,1)S(1)} %collective-permute-done.7.refs_0_.refs_7_), channel_id=1, source_target_pairs={{0,1},{1,0},{2,3},{3,2},{4,5},{5,4},{6,7},{7,6},{8,9},{9,8},{10,11... | collective-permute-start | bytes 258056 | tf_op jit(solution)/shard_map/ppermute | solution.py:261

commit v4 on v3

--- a/solution.py
+++ b/solution.py
@@ -14,7 +14,7 @@
 PRODUCT_LIMIT = 10 * 1024 * 1024
 SHARES = 8
 BANKS = 4
-COLUMNS = 1024
+COLUMNS = 512
 WIRE = jnp.float16
 VMEM = pl.BlockSpec(memory_space=pltpu.VMEM)
 HBM = pl.BlockSpec(memory_space=pltpu.HBM)
@@ -115,11 +115,6 @@
         out_specs=[VMEM] * len(outs),
         compiler_params=params(),
     )(*args)
-
-
-def spread_kernel(halves, received, *outs):
-    for k, out in enumerate(outs):
-        out[...] = halves[0, k] + received[k]
 
 
 def sum_kernel(kept, *refs):
@@ -282,7 +277,7 @@
     halves, noise, *banks = forces_call(green_rows, noise_draws, slabs, bands, pack)
     received = send(halves[1], 1, n)
     part = halves.shape[2:]
-    forces, *sent = small_call(spread_kernel, [part] * (SHARES // 2), halves, received)
+    forces, *sent = [halves[0, k] + received[k] for k in range(SHARES // 2)]
     arrived = [send(block, 2 * k + 2, n) for k, block in enumerate(sent)]
     (forces,) = small_call(sum_kernel, [part], forces, *arrived)
     received = None

time: 51.9 us -> 51.7 us (level)
  no operation moved by 1% of the time
where the time goes in v4:
time: 51.7 us; the launch traced here: 51.5 us
  Pallas kernels  25.2 us (49%)
  waiting for transfers between devices  13.9 us (27%)
  starting transfers between devices  11.5 us (22%)
  between operations  0.75 us (1%)
    pallas_call x1, Pallas kernels, forces_call(): pl.pallas_call(functools.partial(forces_kernel, bands, pack), out_shape=(...  15.9 us
    ppermute x13, waiting for transfers between devices, swap(): return lax.ppermute(block, 'chol', [(i, i ^ bit) for i in range(n)])  13.9 us
    ppermute x13, starting transfers between devices, swap(): return lax.ppermute(block, 'chol', [(i, i ^ bit) for i in range(n)])  11.5 us
    pallas_call x4, Pallas kernels, potential_call(): pl.pallas_call(functools.partial(potential_kernel, shares, pack, first, l...  9.13 us
  transfers between devices with their start and end apart: 13, of which 6 were waited for; matrix products, arithmetic and copies ran while one was open for 0% of the time, Pallas kernels for 14%

profile of v4, /device:TPU:0, one launch (start us, length us, event | category | flops | bytes accessed | tf_op | source)
XLA Modules:
  0.0 51.5 jit_solution(13165166256010742255)
XLA Ops:
  0.6 15.9 %shard_map.50 = (f32[2,4,2,160,128]{4,3,2,1,0:T(8,128)S(1)}, f32[1,160,128]{2,1,0:T(8,128)S(1)}, bf16[16,80,4096]{2,1,0:T(8,128)(2,1)S(1)}, bf16[16,80,4096]{2,1...) custom-call(bf16[64,4096]{1,0:T(8,128)(2,1)} %rows_hbm.1, ...), custom_call_target="tpu_custom_call" | custom-call | flops 2684354560 | bytes 41943040 | tf_op jit(solution)/shard_map/pallas_call | solution.py:89
  16.6 0.6 %collective-permute-start = (f16[4,2,160,128]{3,2,1,0:T(8,128)(2,1)S(1)}, f16[4,2,160,128]{3,2,1,0:T(8,128)(2,1)S(1)}, u32[]{:S(2)}, u32[]{:S(2)}) collective-permute-start(f16[4,2,160,128]{3,2,1,0:T(8,128)(2,1)S(1)} %fusion), channel_id=1, source_target_pairs={{0,1},{1,0},{2,3},{3,2},{4,5},{5,4},{6,7},{7,6},{8,9},{9,8},{10,11... | collective-permute-start | bytes 983048 | tf_op jit(solution)/shard_map/ppermute | solution.py:256
  17.1 1.3 %collective-permute-done = f16[4,2,160,128]{3,2,1,0:T(8,128)(2,1)S(1)} collective-permute-done((f16[4,2,160,128]{3,2,1,0:T(8,128)(2,1)S(1)}, f16[4,2,160,128]{3,2,1,0:T(8,128)(2,1)S(1)}, u32[]{:S(2)}, u32[]{:S(2)}) %collective-permute-start) | collective-permute-done | bytes 327712 | tf_op jit(solution)/shard_map/ppermute | solution.py:256
  18.5 0.1 fusion.2
  18.5 4.0 %collective-permute-start.3 = (f16[2,160,128]{2,1,0:T(8,128)(2,1)S(1)}, f16[2,160,128]{2,1,0:T(8,128)(2,1)S(1)}, u32[]{:S(2)}, u32[]{:S(2)}) collective-permute-start(f16[2,160,128]{2,1,0:T(8,128)(2,1)S(1)} %get-tuple-element.18), channel_id=1, source_target_pairs={{0,6},{1,7},{2,4},{3,5},{4,2},{5,3},{6,0},{7,1},{8,14},{9,15},{10,... | collective-permute-start | bytes 245768 | tf_op jit(solution)/shard_map/ppermute | solution.py:256
  22.5 0.5 collective-permute-start.2
  22.9 0.2 collective-permute-start.1
  23.1 2.9 %collective-permute-start.5 = (f32[1,160,128]{2,1,0:T(8,128)S(1)}, f32[1,160,128]{2,1,0:T(8,128)S(1)}, u32[]{:S(2)}, u32[]{:S(2)}) collective-permute-start(f32[1,160,128]{2,1,0:T(8,128)S(1)} %get-tuple-element.11.first), channel_id=1, source_target_pairs={{0,8},{1,9},{2,10},{3,11},{4,12},{5,13},{6,14},{7,15},{8,0},{9,1},... | collective-permute-start | bytes 245768 | tf_op jit(solution)/shard_map/ppermute | solution.py:256
  26.1 2.9 %collective-permute-done.2 = f16[2,160,128]{2,1,0:T(8,128)(2,1)S(1)} collective-permute-done((f16[2,160,128]{2,1,0:T(8,128)(2,1)S(1)}, f16[2,160,128]{2,1,0:T(8,128)(2,1)S(1)}, u32[]{:S(2)}, u32[]{:S(2)}) %collective-permute-start.2) | collective-permute-done | bytes 81952 | tf_op jit(solution)/shard_map/ppermute | solution.py:256
  29.0 0.1 shard_map.51.kept
  29.0 1.6 %collective-permute-start.4 = (f16[2,160,128]{2,1,0:T(8,128)(2,1)S(1)}, f16[2,160,128]{2,1,0:T(8,128)(2,1)S(1)}, u32[]{:S(2)}, u32[]{:S(2)}) collective-permute-start(f16[2,160,128]{2,1,0:T(8,128)(2,1)S(1)} %convert_element_type.39), channel_id=1, source_target_pairs={{0,8},{1,9},{2,10},{3,11},{4,12},{5,13},{6,14},{7,15},{8,0},{9,1},... | collective-permute-start | bytes 245768 | tf_op jit(solution)/shard_map/ppermute | solution.py:256
  30.6 4.7 %collective-permute-done.4 = f16[2,160,128]{2,1,0:T(8,128)(2,1)S(1)} collective-permute-done((f16[2,160,128]{2,1,0:T(8,128)(2,1)S(1)}, f16[2,160,128]{2,1,0:T(8,128)(2,1)S(1)}, u32[]{:S(2)}, u32[]{:S(2)}) %collective-permute-start.4) | collective-permute-done | bytes 81952 | tf_op jit(solution)/shard_map/ppermute | solution.py:256
  35.3 0.1 shard_map.53.refs_0_.refs_1_
  35.4 0.1 collective-permute-start.6
  35.5 0.9 %collective-permute-start.10 = (bf16[336,128]{1,0:T(8,128)(2,1)S(1)}, bf16[336,128]{1,0:T(8,128)(2,1)S(1)}, u32[]{:S(2)}, u32[]{:S(2)}) collective-permute-start(bf16[336,128]{1,0:T(8,128)(2,1)S(1)} %shard_map.53.refs_0_.refs_1_), channel_id=1, source_target_pairs={{0,2},{1,3},{2,0},{3,1},{4,6},{5,7},{6,4},{7,5},{8,10},{9,11},{10,... | collective-permute-start | bytes 258056 | tf_op jit(solution)/shard_map/ppermute | solution.py:256
  36.3 3.6 %collective-permute-done.6.refs_0_.refs_3_ = bf16[336,128]{1,0:T(8,128)(2,1)S(1)} collective-permute-done((bf16[336,128]{1,0:T(8,128)(2,1)S(1)}, bf16[336,128]{1,0:T(8,128)(2,1)S(1)}, u32[]{:S(2)}, u32[]{:S(2)}) %collective-permute-start.6) | collective-permute-done | bytes 86048 | tf_op jit(solution)/shard_map/ppermute | solution.py:256
  40.0 0.4 collective-permute-start.7
  40.4 0.2 collective-permute-done.10.refs_1_.refs_4_
  40.6 0.5 collective-permute-start.11
  41.1 2.1 %shard_map.54.refs_8_ = f32[64,4096]{1,0:T(8,128)S(1)} custom-call(bf16[336,128]{1,0:T(8,128)(2,1)S(1)} %shard_map.53.refs_0_.refs_1_, bf16[336,128]{1,0:T(8,128)(2,1)S(1)} %collective-permute-done.9.refs_1_.refs_2_, bf16[16,80,4096]{2,1,0:T(8,128)(2,1)S(1)} %get-tuple-element.12.refs_2_.refs_4_.refs_1_.refs_8_, ...), custom_call_target="tpu_custom_call" | custom-call | flops 671088640 | bytes 10485760 | tf_op jit(solution)/shard_map/pallas_call | solution.py:242
  43.2 1.2 %collective-permute-done.7.refs_0_.refs_7_ = bf16[336,128]{1,0:T(8,128)(2,1)S(1)} collective-permute-done((bf16[336,128]{1,0:T(8,128)(2,1)S(1)}, bf16[336,128]{1,0:T(8,128)(2,1)S(1)}, u32[]{:S(2)}, u32[]{:S(2)}) %collective-permute-start.7) | collective-permute-done | bytes 86048 | tf_op jit(solution)/shard_map/ppermute | solution.py:256
  44.5 4.0 %shard_map.55.refs_5_ = f32[64,4096]{1,0:T(8,128)S(1)} custom-call(bf16[336,128]{1,0:T(8,128)(2,1)S(1)} %collective-permute-done.6.refs_0_.refs_3_, bf16[336,128]{1,0:T(8,128)(2,1)S(1)} %collective-permute-done.10.refs_1_.refs_4_, bf16[336,128]{1,0:T(8,128)(2,1)S(1)} %collective-permute-done.11.refs_2_.refs_5_, ...), custom_call_target="tpu_custom_call" | custom-call | flops 1342177280 | bytes 20971520 | tf_op jit(solution)/shard_map/pallas_call | solution.py:242
  48.5 1.1 %shard_map.56.refs_12_ = f32[64,4096]{1,0:T(8,128)S(1)} custom-call(bf16[336,128]{1,0:T(8,128)(2,1)S(1)} %collective-permute-done.7.refs_0_.refs_7_, bf16[16,80,4096]{2,1,0:T(8,128)(2,1)S(1)} %get-tuple-element.12.refs_2_.refs_4_.refs_1_.refs_8_, bf16[16,80,4096]{2,1,0:T(8,128)(2,1)S(1)} %get-tuple-element.13.refs_3_.refs_5_.refs_2_.refs_9_, ...), custom_call_target="tpu_custom_call" | custom-call | flops 335544320 | bytes 5242880 | tf_op jit(solution)/shard_map/pallas_call | solution.py:242
  49.6 1.9 %shard_map.57 = (f32[64,4096]{1,0:T(8,128)}, f32[1,4]{1,0:T(1,128)}) custom-call(bf16[336,128]{1,0:T(8,128)(2,1)S(1)} %collective-permute-done.8.refs_0_, bf16[336,128]{1,0:T(8,128)(2,1)S(1)} %shard_map.53.refs_0_.refs_1_, bf16[336,128]{1,0:T(8,128)(2,1)S(1)} %collective-permute-done.9.refs_1_.refs_2_, ...), custom_call_target="tpu_custom_call" | custom-call | flops 335544320 | bytes 5242880 | tf_op jit(solution)/shard_map/pallas_call | solution.py:242
  (18 shorter events, 0.2 us)
Async XLA Ops:
  16.6 1.8 %collective-permute-start = (f16[4,2,160,128]{3,2,1,0:T(8,128)(2,1)S(1)}, f16[4,2,160,128]{3,2,1,0:T(8,128)(2,1)S(1)}, u32[]{:S(2)}, u32[]{:S(2)}) collective-permute-start(f16[4,2,160,128]{3,2,1,0:T(8,128)(2,1)S(1)} %fusion), channel_id=1, source_target_pairs={{0,1},{1,0},{2,3},{3,2},{4,5},{5,4},{6,7},{7,6},{8,9},{9,8},{10,11... | collective-permute-start | bytes 983048 | tf_op jit(solution)/shard_map/ppermute | solution.py:256
  18.5 7.5 %collective-permute-start.3 = (f16[2,160,128]{2,1,0:T(8,128)(2,1)S(1)}, f16[2,160,128]{2,1,0:T(8,128)(2,1)S(1)}, u32[]{:S(2)}, u32[]{:S(2)}) collective-permute-start(f16[2,160,128]{2,1,0:T(8,128)(2,1)S(1)} %get-tuple-element.18), channel_id=1, source_target_pairs={{0,6},{1,7},{2,4},{3,5},{4,2},{5,3},{6,0},{7,1},{8,14},{9,15},{10,... | collective-permute-start | bytes 245768 | tf_op jit(solution)/shard_map/ppermute | solution.py:256
  22.5 6.4 %collective-permute-start.2 = (f16[2,160,128]{2,1,0:T(8,128)(2,1)S(1)}, f16[2,160,128]{2,1,0:T(8,128)(2,1)S(1)}, u32[]{:S(2)}, u32[]{:S(2)}) collective-permute-start(f16[2,160,128]{2,1,0:T(8,128)(2,1)S(1)} %get-tuple-element.19), channel_id=1, source_target_pairs={{0,4},{1,5},{2,6},{3,7},{4,0},{5,1},{6,2},{7,3},{8,12},{9,13},{10,... | collective-permute-start | bytes 245768 | tf_op jit(solution)/shard_map/ppermute | solution.py:256
  22.9 6.0 %collective-permute-start.1 = (f16[2,160,128]{2,1,0:T(8,128)(2,1)S(1)}, f16[2,160,128]{2,1,0:T(8,128)(2,1)S(1)}, u32[]{:S(2)}, u32[]{:S(2)}) collective-permute-start(f16[2,160,128]{2,1,0:T(8,128)(2,1)S(1)} %get-tuple-element.20), channel_id=1, source_target_pairs={{0,2},{1,3},{2,0},{3,1},{4,6},{5,7},{6,4},{7,5},{8,10},{9,11},{10,... | collective-permute-start | bytes 245768 | tf_op jit(solution)/shard_map/ppermute | solution.py:256
  23.1 7.5 %collective-permute-start.5 = (f32[1,160,128]{2,1,0:T(8,128)S(1)}, f32[1,160,128]{2,1,0:T(8,128)S(1)}, u32[]{:S(2)}, u32[]{:S(2)}) collective-permute-start(f32[1,160,128]{2,1,0:T(8,128)S(1)} %get-tuple-element.11.first), channel_id=1, source_target_pairs={{0,8},{1,9},{2,10},{3,11},{4,12},{5,13},{6,14},{7,15},{8,0},{9,1},... | collective-permute-start | bytes 245768 | tf_op jit(solution)/shard_map/ppermute | solution.py:256
  29.0 6.3 %collective-permute-start.4 = (f16[2,160,128]{2,1,0:T(8,128)(2,1)S(1)}, f16[2,160,128]{2,1,0:T(8,128)(2,1)S(1)}, u32[]{:S(2)}, u32[]{:S(2)}) collective-permute-start(f16[2,160,128]{2,1,0:T(8,128)(2,1)S(1)} %convert_element_type.39), channel_id=1, source_target_pairs={{0,8},{1,9},{2,10},{3,11},{4,12},{5,13},{6,14},{7,15},{8,0},{9,1},... | collective-permute-start | bytes 245768 | tf_op jit(solution)/shard_map/ppermute | solution.py:256
  35.4 4.5 %collective-permute-start.6 = (bf16[336,128]{1,0:T(8,128)(2,1)S(1)}, bf16[336,128]{1,0:T(8,128)(2,1)S(1)}, u32[]{:S(2)}, u32[]{:S(2)}) collective-permute-start(bf16[336,128]{1,0:T(8,128)(2,1)S(1)} %shard_map.53.refs_0_.refs_1_), channel_id=1, source_target_pairs={{0,4},{1,5},{2,6},{3,7},{4,0},{5,1},{6,2},{7,3},{8,12},{9,13},{10,... | collective-permute-start | bytes 258056 | tf_op jit(solution)/shard_map/ppermute | solution.py:256
  35.5 5.1 %collective-permute-start.10 = (bf16[336,128]{1,0:T(8,128)(2,1)S(1)}, bf16[336,128]{1,0:T(8,128)(2,1)S(1)}, u32[]{:S(2)}, u32[]{:S(2)}) collective-permute-start(bf16[336,128]{1,0:T(8,128)(2,1)S(1)} %shard_map.53.refs_0_.refs_1_), channel_id=1, source_target_pairs={{0,2},{1,3},{2,0},{3,1},{4,6},{5,7},{6,4},{7,5},{8,10},{9,11},{10,... | collective-permute-start | bytes 258056 | tf_op jit(solution)/shard_map/ppermute | solution.py:256
  36.3 4.8 %collective-permute-start.9 = (bf16[336,128]{1,0:T(8,128)(2,1)S(1)}, bf16[336,128]{1,0:T(8,128)(2,1)S(1)}, u32[]{:S(2)}, u32[]{:S(2)}) collective-permute-start(bf16[336,128]{1,0:T(8,128)(2,1)S(1)} %shard_map.53.refs_0_.refs_1_), channel_id=1, source_target_pairs={{0,1},{1,0},{2,3},{3,2},{4,5},{5,4},{6,7},{7,6},{8,9},{9,8},{10,11... | collective-permute-start | bytes 258056 | tf_op jit(solution)/shard_map/ppermute | solution.py:256
  40.0 4.5 %collective-permute-start.7 = (bf16[336,128]{1,0:T(8,128)(2,1)S(1)}, bf16[336,128]{1,0:T(8,128)(2,1)S(1)}, u32[]{:S(2)}, u32[]{:S(2)}) collective-permute-start(bf16[336,128]{1,0:T(8,128)(2,1)S(1)} %collective-permute-done.6.refs_0_.refs_3_), channel_id=1, source_target_pairs={{0,2},{1,3},{2,0},{3,1},{4,6},{5,7},{6,4},{7,5},{8,10},{9,11},{10,... | collective-permute-start | bytes 258056 | tf_op jit(solution)/shard_map/ppermute | solution.py:256
  40.6 3.8 %collective-permute-start.12 = (bf16[336,128]{1,0:T(8,128)(2,1)S(1)}, bf16[336,128]{1,0:T(8,128)(2,1)S(1)}, u32[]{:S(2)}, u32[]{:S(2)}) collective-permute-start(bf16[336,128]{1,0:T(8,128)(2,1)S(1)} %collective-permute-done.10.refs_1_.refs_4_), channel_id=1, source_target_pairs={{0,1},{1,0},{2,3},{3,2},{4,5},{5,4},{6,7},{7,6},{8,9},{9,8},{10,11... | collective-permute-start | bytes 258056 | tf_op jit(solution)/shard_map/ppermute | solution.py:256
  40.6 3.8 %collective-permute-start.11 = (bf16[336,128]{1,0:T(8,128)(2,1)S(1)}, bf16[336,128]{1,0:T(8,128)(2,1)S(1)}, u32[]{:S(2)}, u32[]{:S(2)}) collective-permute-start(bf16[336,128]{1,0:T(8,128)(2,1)S(1)} %collective-permute-done.6.refs_0_.refs_3_), channel_id=1, source_target_pairs={{0,1},{1,0},{2,3},{3,2},{4,5},{5,4},{6,7},{7,6},{8,9},{9,8},{10,11... | collective-permute-start | bytes 258056 | tf_op jit(solution)/shard_map/ppermute | solution.py:256
  44.4 5.2 %collective-permute-start.8 = (bf16[336,128]{1,0:T(8,128)(2,1)S(1)}, bf16[336,128]{1,0:T(8,128)(2,1)S(1)}, u32[]{:S(2)}, u32[]{:S(2)}) collective-permute-start(bf16[336,128]{1,0:T(8,128)(2,1)S(1)} %collective-permute-done.7.refs_0_.refs_7_), channel_id=1, source_target_pairs={{0,1},{1,0},{2,3},{3,2},{4,5},{5,4},{6,7},{7,6},{8,9},{9,8},{10,11... | collective-permute-start | bytes 258056 | tf_op jit(solution)/shard_map/ppermute | solution.py:256
